TPU v7x, 32 devices: a whole 2x2x4 slice. The times are simulated.
32 devices in a mesh: row: 4 (over x, core), col: 8 (over z, y).
Axes of the slice: x: 2, y: 2, z: 4, core: 2. Of those that a mesh axis runs over, the one named last changes fastest.
Arguments:
- object_tiles: float32 [2, 2, 1024, 2048], P(None, None, 'row', 'col'), may hold values from -5 to 5
- probe_modes: float32 [2, 2, 128, 128], replicated, may hold values from -4 to 4
- home_offset: int32 [4, 8, 2, 2], P('row', 'col'), may hold values from 0 to 256
- home_amp: bfloat16 [4, 8, 2, 128, 128], P('row', 'col'), may hold values from 0.19921875 to 1.796875
- sur_offset: int32 [4, 8, 2, 4], P('row', 'col'), may hold values from 0 to 256
- sur_helper: int32 [4, 8, 4], P('row', 'col'), may hold values from -1 to 31, as said below
- help_amp: bfloat16 [4, 8, 4, 128, 128], P('row', 'col'), may hold values from 0.19921875 to 1.796875
Outputs:
- object_grad: float32 [2, 2, 1024, 2048], P(None, None, 'row', 'col')
Inputs may be any that keep to these rules, and one draw needn't show every extreme that they name: `sur_helper`: every id that is not -1 is the device at the same tile row and tile column c + 1 or c - 1 (taken modulo 8), as row index times 8 plus column index. No tile sends more than 2 slots to one helper; in every draw some device receives 2 from both column neighbours.
All inputs are finite; a program needn't handle non-finite values.
Results may differ from a plain program's by a relative error of at most 0.0003.
Values may be sent and summed in bfloat16 or wider, within the bound.
A program may use at most 64 MiB of HBM per device.

v0:
```python
import math

import jax
import jax.numpy as jnp
from jax import lax
from jax.sharding import PartitionSpec as P

MARGIN = 64


smooth_eps = 0.1


def padded_2(array, sides, width):
    for axis, dim in sides:
        size, length = (lax.axis_size(axis), array.shape[dim])
        up = [(i, (i + 1) % size) for i in range(size - 1)]
        down = [(j, i) for i, j in up]
        last = lax.slice_in_dim(array, length - width, length, axis=dim)
        leading = lax.slice_in_dim(array, 0, width, axis=dim)
        before = lax.ppermute(last, axis, up)
        after = lax.ppermute(leading, axis, down)
        array = jnp.concatenate([before, array, after], axis=dim)
    return array


def passed_along(block, axis, distance):
    devices = range(lax.axis_size(axis))
    route = [((i - distance) % len(devices), i) for i in devices]
    return lax.ppermute(block, axis, route)


def spectral_tables(width):
    index = jnp.arange(width, dtype=jnp.int32)
    product = index[:, None] * index[None, :] % width
    angle = -2.0 * math.pi / width * product.astype(jnp.float32)
    norm_factor = 1.0 / math.sqrt(width)
    freq = (index - width * (index >= width // 2).astype(jnp.int32)).astype(jnp.float32)
    phase = -math.pi / width * (freq[:, None] ** 2 + freq[None, :] ** 2)
    return (
        jnp.cos(angle) * norm_factor,
        jnp.sin(angle) * norm_factor,
        jnp.cos(phase),
        jnp.sin(phase),
    )


def right_product(left_side, right_side):
    return jnp.matmul(left_side, right_side, precision=lax.Precision.HIGHEST)


def transform(real_part, imag_part, cos_table, sin_table):
    first_real = right_product(real_part, cos_table) - right_product(imag_part, sin_table)
    first_imag = right_product(real_part, sin_table) + right_product(imag_part, cos_table)
    out_real = right_product(cos_table, first_real) - right_product(sin_table, first_imag)
    out_imag = right_product(cos_table, first_imag) + right_product(sin_table, first_real)
    return (out_real, out_imag)


def patch_loss(patch, probe_modes, amplitude, weight, tables):
    cos_table, sin_table, prop_real, prop_imag = tables
    probe_real, probe_imag = (probe_modes[0], probe_modes[1])
    obj_real, obj_imag = (patch[0], patch[1])
    wave_real = probe_real * obj_real[0] - probe_imag * obj_imag[0]
    wave_imag = probe_real * obj_imag[0] + probe_imag * obj_real[0]
    spec_real, spec_imag = transform(wave_real, wave_imag, cos_table, sin_table)
    moved_real = spec_real * prop_real - spec_imag * prop_imag
    moved_imag = spec_real * prop_imag + spec_imag * prop_real
    back_real, back_imag = transform(moved_real, moved_imag, cos_table, -sin_table)
    wave_real = back_real * obj_real[1] - back_imag * obj_imag[1]
    wave_imag = back_real * obj_imag[1] + back_imag * obj_real[1]
    far_real, far_imag = transform(wave_real, wave_imag, cos_table, sin_table)
    intensity = jnp.sum(far_real * far_real + far_imag * far_imag, axis=0)
    misfit = jnp.sqrt(intensity + smooth_eps) - amplitude
    return weight * jnp.sum(misfit * misfit)


def cut_patches(extended, rows_at, cols_at, window):
    zero = jnp.zeros((), jnp.int32)

    def cut_one(row_at, col_at):
        return lax.dynamic_slice(
            extended,
            (zero, zero, row_at, col_at),
            (extended.shape[0], extended.shape[1], window, window),
        )

    return jax.vmap(cut_one)(rows_at, cols_at)


def add_patches(total, grads, rows_at, cols_at):
    zero = jnp.zeros((), jnp.int32)

    def add_one(item, acc):
        piece = grads[item]
        current = lax.dynamic_slice(acc, (zero, zero, rows_at[item], cols_at[item]), piece.shape)
        return lax.dynamic_update_slice(
            acc, current + piece, (zero, zero, rows_at[item], cols_at[item])
        )

    return lax.fori_loop(0, grads.shape[0], add_one, total)


def fold_axis(padded, axis_index, tile, margin):
    core = lax.slice_in_dim(padded, 2 * margin, 2 * margin + tile, axis=axis_index)
    lower = lax.slice_in_dim(padded, 0, margin, axis=axis_index)
    upper = lax.slice_in_dim(padded, tile + 3 * margin, tile + 4 * margin, axis=axis_index)
    lower_pad = [(0, 0)] * padded.ndim
    upper_pad = [(0, 0)] * padded.ndim
    lower_pad[axis_index] = (0, tile - margin)
    upper_pad[axis_index] = (tile - margin, 0)
    return core + jnp.pad(lower, lower_pad) + jnp.pad(upper, upper_pad)


def shards(object_tiles, probe_modes, home_offset, home_amp, sur_offset, sur_helper, help_amp):
    window = probe_modes.shape[-1]
    tile = object_tiles.shape[-1]
    tables = spectral_tables(window)
    patch_gradient = jax.vmap(jax.grad(patch_loss), in_axes=(0, None, 0, 0, None))
    extended = padded_2(object_tiles, (("row", 2), ("col", 3)), MARGIN)
    home_rows = home_offset[0, 0, 0]
    home_cols = home_offset[0, 0, 1]
    home_patches = cut_patches(extended, home_rows, home_cols, window)
    home_grads = patch_gradient(
        home_patches,
        probe_modes,
        home_amp[0, 0].astype(jnp.float32),
        jnp.ones(home_rows.shape, jnp.float32),
        tables,
    )
    helper = sur_helper[0, 0]
    columns = lax.axis_size("col")
    my_column = lax.axis_index("col")
    helper_column = helper % columns
    live = helper >= 0
    to_right = live & (helper_column == (my_column + 1) % columns)
    to_left = live & jnp.logical_not(to_right)
    right_rank = jnp.cumsum(to_right.astype(jnp.int32)) - 1
    left_rank = jnp.cumsum(to_left.astype(jnp.int32)) - 1
    half_slots = help_amp.shape[2] // 2
    slot_ids = jnp.arange(half_slots, dtype=jnp.int32)
    select_right = ((right_rank[None, :] == slot_ids[:, None]) & to_right[None, :]).astype(
        jnp.float32
    )
    select_left = ((left_rank[None, :] == slot_ids[:, None]) & to_left[None, :]).astype(jnp.float32)
    sur_rows = sur_offset[0, 0, 0]
    sur_cols = sur_offset[0, 0, 1]
    sur_patches = cut_patches(extended, sur_rows, sur_cols, window)
    highest = lax.Precision.HIGHEST
    amps_right = passed_along(help_amp[0, 0, :half_slots], "col", -1)
    amps_left = passed_along(help_amp[0, 0, half_slots:], "col", 1)
    sur_amps = jnp.einsum(
        "js,jxy->sxy", select_right, amps_right.astype(jnp.float32), precision=highest
    ) + jnp.einsum("js,jxy->sxy", select_left, amps_left.astype(jnp.float32), precision=highest)
    sur_grads = patch_gradient(sur_patches, probe_modes, sur_amps, live.astype(jnp.float32), tables)
    all_grads = jnp.concatenate([home_grads, sur_grads], axis=0)
    all_rows = jnp.concatenate([home_rows, sur_rows])
    all_cols = jnp.concatenate([home_cols, sur_cols])
    extended_grad = add_patches(jnp.zeros_like(extended), all_grads, all_rows, all_cols)
    row_padded = padded_2(extended_grad, (("row", 2),), MARGIN)
    row_folded = fold_axis(row_padded, 2, tile, MARGIN)
    col_padded = padded_2(row_folded, (("col", 3),), MARGIN)
    return fold_axis(col_padded, 3, tile, MARGIN)


def solution(mesh):
    return jax.shard_map(
        shards,
        mesh=mesh,
        in_specs=(
            P(None, None, "row", "col"),
            P(),
            P("row", "col", None, None),
            P("row", "col", None, None, None),
            P("row", "col", None, None),
            P("row", "col", None),
            P("row", "col", None, None, None),
        ),
        out_specs=P(None, None, "row", "col"),
        check_vma=False,
    )
```

profile of v0, /device:TPU:9, one launch (start us, length us, event | category | flops | bytes accessed | tf_op | source)
XLA Modules:
  0.0 240.5 jit_solution(476973030611061066)
XLA Ops:
  0.0 1.6 copy.124
  2.8 3.7 %collective-permute-start = (f32[2,2,64,256]{2,3,1,0:T(8,128)}, f32[2,2,64,256]{2,3,1,0:T(8,128)S(1)}, u32[]{:S(2)}, u32[]{:S(2)}) collective-permute-start(f32[2,2,64,256]{2,3,1,0:T(8,128)} %get-tuple-element.194), channel_id=1, source_target_pairs={{0,8},{8,16},{16,24},{1,9},{9,17},{17,25},{2,10},{10,18},{18,26},{... | collective-permute-start | bytes 786440 | tf_op jit(solution)/shard_map/ppermute | solution.py:21
  6.5 1.9 collective-permute-start.1
  14.8 2.4 %collective-permute-done.1 = f32[2,2,64,256]{2,3,1,0:T(8,128)S(1)} collective-permute-done((f32[2,2,64,256]{2,3,1,0:T(8,128)}, f32[2,2,64,256]{2,3,1,0:T(8,128)S(1)}, u32[]{:S(2)}, u32[]{:S(2)}) %collective-permute-start.1) | collective-permute-done | bytes 262176 | tf_op jit(solution)/shard_map/ppermute | solution.py:22
  17.6 3.1 %collective-permute-start.2 = (f32[2,2,384,64]{2,3,1,0:T(8,128)S(1)}, f32[2,2,384,64]{2,3,1,0:T(8,128)S(1)}, u32[]{:S(2)}, u32[]{:S(2)}) collective-permute-start(f32[2,2,384,64]{2,3,1,0:T(8,128)S(1)} %get-tuple-element.188), channel_id=1, source_target_pairs={{0,1},{1,2},{2,3},{3,4},{4,5},{5,6},{6,7},{8,9},{9,10},{10,11},{11... | collective-permute-start | bytes 1179656 | tf_op jit(solution)/shard_map/ppermute | solution.py:21
  20.7 3.0 %collective-permute-start.3 = (f32[2,2,384,64]{2,3,1,0:T(8,128)S(1)}, f32[2,2,384,64]{2,3,1,0:T(8,128)S(1)}, u32[]{:S(2)}, u32[]{:S(2)}) collective-permute-start(f32[2,2,384,64]{2,3,1,0:T(8,128)S(1)} %get-tuple-element.189), channel_id=1, source_target_pairs={{1,0},{2,1},{3,2},{4,3},{5,4},{6,5},{7,6},{9,8},{10,9},{11,10},{12... | collective-permute-start | bytes 1179656 | tf_op jit(solution)/shard_map/ppermute | solution.py:22
  25.7 8.1 %collective-permute-done.2 = f32[2,2,384,64]{2,3,1,0:T(8,128)S(1)} collective-permute-done((f32[2,2,384,64]{2,3,1,0:T(8,128)S(1)}, f32[2,2,384,64]{2,3,1,0:T(8,128)S(1)}, u32[]{:S(2)}, u32[]{:S(2)}) %collective-permute-start.2) | collective-permute-done | bytes 393248 | tf_op jit(solution)/shard_map/ppermute | solution.py:21
  33.9 2.7 %collective-permute-done.3 = f32[2,2,384,64]{2,3,1,0:T(8,128)S(1)} collective-permute-done((f32[2,2,384,64]{2,3,1,0:T(8,128)S(1)}, f32[2,2,384,64]{2,3,1,0:T(8,128)S(1)}, u32[]{:S(2)}, u32[]{:S(2)}) %collective-permute-start.3) | collective-permute-done | bytes 393248 | tf_op jit(solution)/shard_map/ppermute | solution.py:22
  36.5 2.0 pad_maximum_fusion
  38.6 2.0 copy.129
  40.6 4.6 %while.16 = (s32[]{:T(128)}, f32[2,2,384,384]{3,2,1,0:T(8,128)S(1)}, s32[2,4]{1,0:T(2,128)S(1)}, f32[2,2,2,128,128]{4,3,2,1,0:T(8,128)S(1)}, s32[]{:T(128)}) while((s32[]{:T(128)}, f32[2,2,384,384]{3,2,1,0:T(8,128)S(1)}, s32[2,4]{1,0:T(2,128)S(1)}, f32[2,2,2,128,128]{4,3,2,1,0:T(8,128)S(1)}, s32[]{:T(128)}) %tuple.113), condition=%wide.while_cond, body=%wide.while_body.sunk | while | flops 2 | bytes 524413 | solution.py:82
  66.4 1.5 multiply_reduce_fusion.15
  79.3 11.5 %while.17 = (s32[]{:T(128)}, f32[2,2,384,384]{3,2,1,0:T(8,128)S(1)}, s32[4,4]{1,0:T(4,128)S(1)}, f32[4,2,2,128,128]{4,3,2,1,0:T(8,128)}, s32[]{:T(128)}) while((s32[]{:T(128)}, f32[2,2,384,384]{3,2,1,0:T(8,128)S(1)}, s32[4,4]{1,0:T(4,128)S(1)}, f32[4,2,2,128,128]{4,3,2,1,0:T(8,128)}, s32[]{:T(128)}) %tuple.112), condition=%wide.while_cond.1, body=%wide.while_body.1.sunk | while | flops 2 | bytes 525937 | solution.py:82
  80.0 2.2 bitcast_dynamic-update-slice_fusion.5
  82.8 2.2 bitcast_dynamic-update-slice_fusion.5
  85.7 2.2 bitcast_dynamic-update-slice_fusion.5
  88.6 2.2 bitcast_dynamic-update-slice_fusion.5
  146.2 57.7 %while.15 = (s32[]{:T(128)}, f32[2,2,384,384]{3,2,1,0:T(8,128)S(1)}, s32[6]{0:T(128)S(1)}, s32[6]{0:T(128)S(1)}, f32[6,2,2,128,128]{4,3,2,1,0:T(8,128)}, /*index=5*/s32[]{:T(128)}, s32[]{:T(128)}, s32[]{:T(128)}) while((s32[]{:T(128)}, f32[2,2,384,384]{3,2,1,0:T(8,128)S(1)}, s32[6]{0:T(128)S(1)}, s32[6]{0:T(128)S(1)}, ...), condition=%wide.region_21.22_spmd, body=%wide.region_20.21_spmd.sunk | while | flops 65544 | bytes 1310913 | solution.py:101
  152.4 3.4 %dynamic_update_slice.8 = f32[2,2,384,384]{3,2,1,0:T(8,128)S(1)} dynamic-update-slice(f32[2,2,384,384]{3,2,1,0:T(8,128)S(1)} %get-tuple-element.361, f32[2,2,128,128]{3,2,1,0:T(8,128)S(1)} %bitcast_add_fusion.2, s32[]{:T(128)} %constant.91.clone.1..sunk, s32[]{:T(128)} %constant.91.clone.1..sunk, s32[]{:T(128)S(6)} %select_n.631, s32[]{:T(128)S(6)} %select_n.632) | dynamic-update-slice | bytes 524292 | tf_op jit(solution)/shard_map/while/body/eval_jaxpr/dynamic_update_slice | solution.py:97
  162.0 3.4 %dynamic_update_slice.8 = f32[2,2,384,384]{3,2,1,0:T(8,128)S(1)} dynamic-update-slice(f32[2,2,384,384]{3,2,1,0:T(8,128)S(1)} %get-tuple-element.361, f32[2,2,128,128]{3,2,1,0:T(8,128)S(1)} %bitcast_add_fusion.2, s32[]{:T(128)} %constant.91.clone.1..sunk, s32[]{:T(128)} %constant.91.clone.1..sunk, s32[]{:T(128)S(6)} %select_n.631, s32[]{:T(128)S(6)} %select_n.632) | dynamic-update-slice | bytes 524292 | tf_op jit(solution)/shard_map/while/body/eval_jaxpr/dynamic_update_slice | solution.py:97
  171.6 3.4 %dynamic_update_slice.8 = f32[2,2,384,384]{3,2,1,0:T(8,128)S(1)} dynamic-update-slice(f32[2,2,384,384]{3,2,1,0:T(8,128)S(1)} %get-tuple-element.361, f32[2,2,128,128]{3,2,1,0:T(8,128)S(1)} %bitcast_add_fusion.2, s32[]{:T(128)} %constant.91.clone.1..sunk, s32[]{:T(128)} %constant.91.clone.1..sunk, s32[]{:T(128)S(6)} %select_n.631, s32[]{:T(128)S(6)} %select_n.632) | dynamic-update-slice | bytes 524292 | tf_op jit(solution)/shard_map/while/body/eval_jaxpr/dynamic_update_slice | solution.py:97
  181.3 3.4 %dynamic_update_slice.8 = f32[2,2,384,384]{3,2,1,0:T(8,128)S(1)} dynamic-update-slice(f32[2,2,384,384]{3,2,1,0:T(8,128)S(1)} %get-tuple-element.361, f32[2,2,128,128]{3,2,1,0:T(8,128)S(1)} %bitcast_add_fusion.2, s32[]{:T(128)} %constant.91.clone.1..sunk, s32[]{:T(128)} %constant.91.clone.1..sunk, s32[]{:T(128)S(6)} %select_n.631, s32[]{:T(128)S(6)} %select_n.632) | dynamic-update-slice | bytes 524292 | tf_op jit(solution)/shard_map/while/body/eval_jaxpr/dynamic_update_slice | solution.py:97
  190.9 3.4 %dynamic_update_slice.8 = f32[2,2,384,384]{3,2,1,0:T(8,128)S(1)} dynamic-update-slice(f32[2,2,384,384]{3,2,1,0:T(8,128)S(1)} %get-tuple-element.361, f32[2,2,128,128]{3,2,1,0:T(8,128)S(1)} %bitcast_add_fusion.2, s32[]{:T(128)} %constant.91.clone.1..sunk, s32[]{:T(128)} %constant.91.clone.1..sunk, s32[]{:T(128)S(6)} %select_n.631, s32[]{:T(128)S(6)} %select_n.632) | dynamic-update-slice | bytes 524292 | tf_op jit(solution)/shard_map/while/body/eval_jaxpr/dynamic_update_slice | solution.py:97
  200.5 3.4 %dynamic_update_slice.8 = f32[2,2,384,384]{3,2,1,0:T(8,128)S(1)} dynamic-update-slice(f32[2,2,384,384]{3,2,1,0:T(8,128)S(1)} %get-tuple-element.361, f32[2,2,128,128]{3,2,1,0:T(8,128)S(1)} %bitcast_add_fusion.2, s32[]{:T(128)} %constant.91.clone.1..sunk, s32[]{:T(128)} %constant.91.clone.1..sunk, s32[]{:T(128)S(6)} %select_n.631, s32[]{:T(128)S(6)} %select_n.632) | dynamic-update-slice | bytes 524292 | tf_op jit(solution)/shard_map/while/body/eval_jaxpr/dynamic_update_slice | solution.py:97
  204.0 1.9 collective-permute-start.6
  205.9 2.4 %collective-permute-start.7 = (f32[2,2,64,384]{3,2,1,0:T(8,128)S(1)}, f32[2,2,64,384]{3,2,1,0:T(8,128)S(1)}, u32[]{:S(2)}, u32[]{:S(2)}) collective-permute-start(f32[2,2,64,384]{3,2,1,0:T(8,128)S(1)} %get-tuple-element.187), channel_id=1, source_target_pairs={{8,0},{16,8},{24,16},{9,1},{17,9},{25,17},{10,2},{18,10},{26,18},{... | collective-permute-start | bytes 1179656 | tf_op jit(solution)/shard_map/ppermute | solution.py:22
  208.3 2.3 collective-permute-done.6
  210.6 4.4 %collective-permute-done.7 = f32[2,2,64,384]{3,2,1,0:T(8,128)S(1)} collective-permute-done((f32[2,2,64,384]{3,2,1,0:T(8,128)S(1)}, f32[2,2,64,384]{3,2,1,0:T(8,128)S(1)}, u32[]{:S(2)}, u32[]{:S(2)}) %collective-permute-start.7) | collective-permute-done | bytes 393248 | tf_op jit(solution)/shard_map/ppermute | solution.py:22
  215.4 2.2 collective-permute-start.8
  217.6 4.0 %collective-permute-start.9 = (f32[2,2,256,64]{3,2,1,0:T(8,128)S(1)}, f32[2,2,256,64]{3,2,1,0:T(8,128)S(1)}, u32[]{:S(2)}, u32[]{:S(2)}) collective-permute-start(f32[2,2,256,64]{3,2,1,0:T(8,128)S(1)} %get-tuple-element.191), channel_id=1, source_target_pairs={{1,0},{2,1},{3,2},{4,3},{5,4},{6,5},{7,6},{9,8},{10,9},{11,10},{12... | collective-permute-start | bytes 786440 | tf_op jit(solution)/shard_map/ppermute | solution.py:22
  221.6 13.9 %collective-permute-done.8 = f32[2,2,256,64]{3,2,1,0:T(8,128)S(1)} collective-permute-done((f32[2,2,256,64]{3,2,1,0:T(8,128)S(1)}, f32[2,2,256,64]{3,2,1,0:T(8,128)S(1)}, u32[]{:S(2)}, u32[]{:S(2)}) %collective-permute-start.8) | collective-permute-done | bytes 262176 | tf_op jit(solution)/shard_map/ppermute | solution.py:21
  235.5 3.3 %collective-permute-done.9 = f32[2,2,256,64]{3,2,1,0:T(8,128)S(1)} collective-permute-done((f32[2,2,256,64]{3,2,1,0:T(8,128)S(1)}, f32[2,2,256,64]{3,2,1,0:T(8,128)S(1)}, u32[]{:S(2)}, u32[]{:S(2)}) %collective-permute-start.9) | collective-permute-done | bytes 262176 | tf_op jit(solution)/shard_map/ppermute | solution.py:22
  (220 shorter events, 119.2 us)
Async XLA Ops:
  0.0 8.4 %copy-start.9 = (bf16[1,1,4,128,128]{4,3,2,1,0:T(8,128)(2,1)S(1)}, bf16[1,1,4,128,128]{4,3,2,1,0:T(8,128)(2,1)}, u32[]{:S(2)}) copy-start(bf16[1,1,4,128,128]{4,3,2,1,0:T(8,128)(2,1)} %param.15) | copy-start | bytes 393220
  0.0 11.1 %copy-start.13 = (s32[1,1,4]{2,1,0:T(1,128)S(1)}, s32[1,1,4]{2,1,0:T(1,128)}, u32[]{:S(2)}) copy-start(s32[1,1,4]{2,1,0:T(1,128)} %param.14) | copy-start | bytes 52
  0.0 11.1 %copy-start.11 = (s32[1,1,2,2]{3,2,1,0:T(2,128)S(1)}, s32[1,1,2,2]{3,2,1,0:T(2,128)}, u32[]{:S(2)}) copy-start(s32[1,1,2,2]{3,2,1,0:T(2,128)} %param.11) | copy-start | bytes 52
  0.0 11.1 %copy-start.12 = (s32[1,1,2,4]{3,2,1,0:T(2,128)S(1)}, s32[1,1,2,4]{3,2,1,0:T(2,128)}, u32[]{:S(2)}) copy-start(s32[1,1,2,4]{3,2,1,0:T(2,128)} %param.13) | copy-start | bytes 100
  0.0 14.7 %copy-start.8 = (f32[2,2,128,128]{3,2,1,0:T(8,128)S(1)}, f32[2,2,128,128]{3,2,1,0:T(8,128)}, u32[]{:S(2)}) copy-start(f32[2,2,128,128]{3,2,1,0:T(8,128)} %param.10) | copy-start | bytes 786436
  2.8 11.9 %collective-permute-start = (f32[2,2,64,256]{2,3,1,0:T(8,128)}, f32[2,2,64,256]{2,3,1,0:T(8,128)S(1)}, u32[]{:S(2)}, u32[]{:S(2)}) collective-permute-start(f32[2,2,64,256]{2,3,1,0:T(8,128)} %get-tuple-element.194), channel_id=1, source_target_pairs={{0,8},{8,16},{16,24},{1,9},{9,17},{17,25},{2,10},{10,18},{18,26},{... | collective-permute-start | bytes 786440 | tf_op jit(solution)/shard_map/ppermute | solution.py:21
  6.5 10.7 %collective-permute-start.1 = (f32[2,2,64,256]{2,3,1,0:T(8,128)}, f32[2,2,64,256]{2,3,1,0:T(8,128)S(1)}, u32[]{:S(2)}, u32[]{:S(2)}) collective-permute-start(f32[2,2,64,256]{2,3,1,0:T(8,128)} %get-tuple-element.195), channel_id=1, source_target_pairs={{8,0},{16,8},{24,16},{9,1},{17,9},{25,17},{10,2},{18,10},{26,18},{... | collective-permute-start | bytes 786440 | tf_op jit(solution)/shard_map/ppermute | solution.py:22
  8.5 15.2 %collective-permute-start.5 = (bf16[2,128,128]{2,0,1:T(2,128)(2,1)S(1)}, bf16[2,128,128]{2,0,1:T(2,128)(2,1)S(1)}, u32[]{:S(2)}, u32[]{:S(2)}) collective-permute-start(bf16[2,128,128]{2,0,1:T(2,128)(2,1)S(1)} %bitcast.533), channel_id=1, source_target_pairs={{7,0},{0,1},{1,2},{2,3},{3,4},{4,5},{5,6},{6,7},{15,8},{8,9},{9,10... | collective-permute-start | bytes 196616 | tf_op jit(solution)/shard_map/ppermute | solution.py:30
  9.9 14.9 %collective-permute-start.4 = (bf16[2,128,128]{2,0,1:T(2,128)(2,1)S(1)}, bf16[2,128,128]{2,0,1:T(2,128)(2,1)S(1)}, u32[]{:S(2)}, u32[]{:S(2)}) collective-permute-start(bf16[2,128,128]{2,0,1:T(2,128)(2,1)S(1)} %bitcast.532), channel_id=1, source_target_pairs={{1,0},{2,1},{3,2},{4,3},{5,4},{6,5},{7,6},{0,7},{9,8},{10,9},{11,1... | collective-permute-start | bytes 196616 | tf_op jit(solution)/shard_map/ppermute | solution.py:30
  14.7 9.0 %copy-start.16 = (s32[4]{0:T(128)S(1)}, s32[4]{0:T(128)}, u32[]{:S(2)}) copy-start(s32[4]{0:T(128)} %add_bitcast_fusion.4) | copy-start | bytes 52
  14.7 10.0 %copy-start.15 = (s32[4]{0:T(128)S(1)}, s32[4]{0:T(128)}, u32[]{:S(2)}) copy-start(s32[4]{0:T(128)} %add_bitcast_fusion.5) | copy-start | bytes 52
  17.6 16.3 %collective-permute-start.2 = (f32[2,2,384,64]{2,3,1,0:T(8,128)S(1)}, f32[2,2,384,64]{2,3,1,0:T(8,128)S(1)}, u32[]{:S(2)}, u32[]{:S(2)}) collective-permute-start(f32[2,2,384,64]{2,3,1,0:T(8,128)S(1)} %get-tuple-element.188), channel_id=1, source_target_pairs={{0,1},{1,2},{2,3},{3,4},{4,5},{5,6},{6,7},{8,9},{9,10},{10,11},{11... | collective-permute-start | bytes 1179656 | tf_op jit(solution)/shard_map/ppermute | solution.py:21
  20.7 15.8 %collective-permute-start.3 = (f32[2,2,384,64]{2,3,1,0:T(8,128)S(1)}, f32[2,2,384,64]{2,3,1,0:T(8,128)S(1)}, u32[]{:S(2)}, u32[]{:S(2)}) collective-permute-start(f32[2,2,384,64]{2,3,1,0:T(8,128)S(1)} %get-tuple-element.189), channel_id=1, source_target_pairs={{1,0},{2,1},{3,2},{4,3},{5,4},{6,5},{7,6},{9,8},{10,9},{11,10},{12... | collective-permute-start | bytes 1179656 | tf_op jit(solution)/shard_map/ppermute | solution.py:22
  38.6 2.0 copy-start.14
  57.5 3.7 %copy-start.10 = (bf16[1,1,2,128,128]{4,3,2,1,0:T(8,128)(2,1)S(1)}, bf16[1,1,2,128,128]{4,3,2,1,0:T(8,128)(2,1)}, u32[]{:S(2)}) copy-start(bf16[1,1,2,128,128]{4,3,2,1,0:T(8,128)(2,1)} %param.12) | copy-start | bytes 196612
  110.3 2.6 %copy-start.1 = (f32[4,128,128]{2,0,1:T(4,128)S(1)}, f32[4,128,128]{2,0,1:T(4,128)}, u32[]{:S(2)}) copy-start(f32[4,128,128]{2,0,1:T(4,128)} %fusion.259) | copy-start | bytes 786436
  110.3 2.6 %copy-start.2 = (f32[4,128,128]{2,0,1:T(4,128)S(1)}, f32[4,128,128]{2,0,1:T(4,128)}, u32[]{:S(2)}) copy-start(f32[4,128,128]{2,0,1:T(4,128)} %fusion.261) | copy-start | bytes 786436
  134.7 3.5 %copy-start = (f32[2,2,128,128]{3,2,1,0:T(8,128)S(1)}, f32[2,2,128,128]{3,2,1,0:T(8,128)}, u32[]{:S(2)}) copy-start(f32[2,2,128,128]{3,2,1,0:T(8,128)} %fusion.45) | copy-start | bytes 786436
  137.1 3.9 %copy-start.3 = (f32[2,2,128,128]{3,2,1,0:T(8,128)S(1)}, f32[2,2,128,128]{3,2,1,0:T(8,128)}, u32[]{:S(2)}) copy-start(f32[2,2,128,128]{3,2,1,0:T(8,128)} %fusion.150) | copy-start | bytes 786436
  139.0 3.0 %copy-start.6 = (f32[2,128,128]{2,1,0:T(8,128)S(1)}, f32[2,128,128]{2,1,0:T(8,128)}, u32[]{:S(2)}) copy-start(f32[2,128,128]{2,1,0:T(8,128)} %get-tuple-element.142) | copy-start | bytes 393220
  139.0 3.0 %copy-start.7 = (f32[2,128,128]{2,1,0:T(8,128)S(1)}, f32[2,128,128]{2,1,0:T(8,128)}, u32[]{:S(2)}) copy-start(f32[2,128,128]{2,1,0:T(8,128)} %get-tuple-element.144) | copy-start | bytes 393220
  139.0 3.1 %copy-start.4 = (f32[2,128,128]{2,1,0:T(8,128)S(1)}, f32[2,128,128]{2,1,0:T(8,128)}, u32[]{:S(2)}) copy-start(f32[2,128,128]{2,1,0:T(8,128)} %get-tuple-element.143) | copy-start | bytes 393220
  139.0 3.0 %copy-start.5 = (f32[2,128,128]{2,1,0:T(8,128)S(1)}, f32[2,128,128]{2,1,0:T(8,128)}, u32[]{:S(2)}) copy-start(f32[2,128,128]{2,1,0:T(8,128)} %get-tuple-element.145) | copy-start | bytes 393220
  144.7 1.5 copy-start.17
  144.7 1.5 copy-start.18
  204.0 6.6 %collective-permute-start.6 = (f32[2,2,64,384]{3,2,1,0:T(8,128)S(1)}, f32[2,2,64,384]{3,2,1,0:T(8,128)S(1)}, u32[]{:S(2)}, u32[]{:S(2)}) collective-permute-start(f32[2,2,64,384]{3,2,1,0:T(8,128)S(1)} %get-tuple-element.186), channel_id=1, source_target_pairs={{0,8},{8,16},{16,24},{1,9},{9,17},{17,25},{2,10},{10,18},{18,26},{... | collective-permute-start | bytes 1179656 | tf_op jit(solution)/shard_map/ppermute | solution.py:21
  205.9 9.1 %collective-permute-start.7 = (f32[2,2,64,384]{3,2,1,0:T(8,128)S(1)}, f32[2,2,64,384]{3,2,1,0:T(8,128)S(1)}, u32[]{:S(2)}, u32[]{:S(2)}) collective-permute-start(f32[2,2,64,384]{3,2,1,0:T(8,128)S(1)} %get-tuple-element.187), channel_id=1, source_target_pairs={{8,0},{16,8},{24,16},{9,1},{17,9},{25,17},{10,2},{18,10},{26,18},{... | collective-permute-start | bytes 1179656 | tf_op jit(solution)/shard_map/ppermute | solution.py:22
  215.4 20.1 %collective-permute-start.8 = (f32[2,2,256,64]{3,2,1,0:T(8,128)S(1)}, f32[2,2,256,64]{3,2,1,0:T(8,128)S(1)}, u32[]{:S(2)}, u32[]{:S(2)}) collective-permute-start(f32[2,2,256,64]{3,2,1,0:T(8,128)S(1)} %get-tuple-element.190), channel_id=1, source_target_pairs={{0,1},{1,2},{2,3},{3,4},{4,5},{5,6},{6,7},{8,9},{9,10},{10,11},{11... | collective-permute-start | bytes 786440 | tf_op jit(solution)/shard_map/ppermute | solution.py:21
  217.6 21.1 %collective-permute-start.9 = (f32[2,2,256,64]{3,2,1,0:T(8,128)S(1)}, f32[2,2,256,64]{3,2,1,0:T(8,128)S(1)}, u32[]{:S(2)}, u32[]{:S(2)}) collective-permute-start(f32[2,2,256,64]{3,2,1,0:T(8,128)S(1)} %get-tuple-element.191), channel_id=1, source_target_pairs={{1,0},{2,1},{3,2},{4,3},{5,4},{6,5},{7,6},{9,8},{10,9},{11,10},{12... | collective-permute-start | bytes 786440 | tf_op jit(solution)/shard_map/ppermute | solution.py:22
where the time goes:
time: 245 us; the launch traced here: 240 us
  matrix products  87 us (36%)
  local copies, waits for them, and re-layouts  50.8 us (21%)
  waiting for transfers between devices  37.1 us (15%)
  starting transfers between devices  24.8 us (10%)
  loops' own time  23.8 us (10%)
  other arithmetic  15.6 us (6%)
    dot_general x96, matrix products, right_product(): return jnp.matmul(left_side, right_side, precision=lax.Precision.HIGHEST)  85 us
    ppermute x4, waiting for transfers between devices, padded_2(): before = lax.ppermute(last, axis, up)  24.3 us
    another operation x1, loops' own time, add_patches(): return lax.fori_loop(0, grads.shape[0], add_one, total)  23.5 us
    dynamic_update_slice x6, local copies, waits for them, and re-layouts, add_one(): lax.dynamic_update_slice(acc, current + piece, (zero, zero, rows_at[item]...  20.5 us
    gather x18, local copies, waits for them, and re-layouts  15.9 us
    ppermute x4, waiting for transfers between devices, padded_2(): after = lax.ppermute(leading, axis, down)  12.8 us
    ppermute x4, starting transfers between devices, padded_2(): after = lax.ppermute(leading, axis, down)  11.3 us
    ppermute x4, starting transfers between devices, padded_2(): before = lax.ppermute(last, axis, up)  11 us
  transfers between devices with their start and end apart: 10, of which 7 were waited for; matrix products, arithmetic and copies ran while one was open for 3% of the time, Pallas kernels for 0%

commit v1 on v0

v1 whole, which is shorter than its diff:
```python
import math

import numpy as np
import ml_dtypes
import jax
import jax.numpy as jnp
from jax import lax
from jax.experimental import pallas as pl
from jax.experimental.pallas import tpu as pltpu
from jax.sharding import PartitionSpec as P

MARGIN = 64
LANES = 128
EPS = 0.1


def shift_along(block, axis, step):
    size = lax.axis_size(axis)
    pairs = [(i, i + step) for i in range(size) if 0 <= i + step < size]
    return lax.ppermute(block, axis, pairs)


def passed_along(block, axis, distance):
    size = lax.axis_size(axis)
    return lax.ppermute(block, axis, [((i - distance) % size, i) for i in range(size)])


def split_tables(window):
    index = np.arange(window)
    spectral = np.exp(-2j * np.pi / window * (index[:, None] * index[None, :] % window))
    spectral /= math.sqrt(window)
    freq = np.where(index >= window // 2, index - window, index).astype(np.float64)
    carrier = np.exp(-1j * np.pi / window * freq**2)
    propagate = np.conj(spectral) @ (carrier[:, None] * spectral)
    blocks = []
    for table in (propagate, spectral):
        blocks += [table.real, table.imag, -table.imag]
    full = np.stack(blocks).astype(np.float32)
    high = full.astype(ml_dtypes.bfloat16)
    low = (full - high.astype(np.float32)).astype(ml_dtypes.bfloat16)
    return np.stack([high, low])


def split(x):
    high = x.astype(jnp.bfloat16)
    low = (x - high.astype(jnp.float32)).astype(jnp.bfloat16)
    return high, low


def square(tab, which, flip):
    def one(part):
        re, im, neg = (tab[part, 3 * which + k] for k in range(3))
        if flip:
            im, neg = neg, im
        top = jnp.concatenate([re, im], axis=1)
        return jnp.concatenate([top, jnp.concatenate([neg, re], axis=1)], axis=0)

    return one(0), one(1)


def dot(a, b):
    return jnp.dot(a, b, preferred_element_type=jnp.float32)


def sandwich(fields, tab, which, conj):
    rows = [jnp.concatenate([re, im], axis=1) for re, im in fields]
    high, low = split(jnp.concatenate(rows, axis=0))
    t_high, t_low = square(tab, which, conj)
    first = dot(
        jnp.concatenate([high, low, high], axis=1),
        jnp.concatenate([t_high, t_high, t_low], axis=0),
    )
    w = first.shape[1] // 2
    count = len(fields)
    top = jnp.concatenate([first[m * w:(m + 1) * w, :w] for m in range(count)], axis=1)
    low_half = jnp.concatenate([first[m * w:(m + 1) * w, w:] for m in range(count)], axis=1)
    high, low = split(jnp.concatenate([top, low_half], axis=0))
    t_high, t_low = square(tab, which, not conj)
    second = dot(
        jnp.concatenate([t_high, t_low, t_high], axis=1),
        jnp.concatenate([high, high, low], axis=0),
    )
    return [
        (second[:w, m * w:(m + 1) * w], second[w:, m * w:(m + 1) * w]) for m in range(count)
    ]


def times(a, b):
    return a[0] * b[0] - a[1] * b[1], a[0] * b[1] + a[1] * b[0]


def conj_times(a, b):
    return a[0] * b[0] + a[1] * b[1], a[0] * b[1] - a[1] * b[0]


def position_gradient(o1, o2, probes, amp, weight, tab):
    waves = sandwich([times(p, o1) for p in probes], tab, 0, False)
    far = sandwich([times(b, o2) for b in waves], tab, 1, False)
    intensity = sum(re * re + im * im for re, im in far)
    factor = (2.0 * weight) * (1.0 - amp * lax.rsqrt(intensity + EPS))
    exits = sandwich([(re * factor, im * factor) for re, im in far], tab, 1, True)
    g2 = [conj_times(b, e) for b, e in zip(waves, exits)]
    entry = sandwich([conj_times(o2, e) for e in exits], tab, 0, True)
    g1 = [conj_times(p, e) for p, e in zip(probes, entry)]
    total = lambda parts: (sum(p[0] for p in parts), sum(p[1] for p in parts))
    return total(g1), total(g2)


def compute_kernel(
    group, where_ref, weight_ref, tab, probe_ref, amp_ref, ext_ref, out_ref, obj, acc
):
    tiles = ext_ref.shape[2] // LANES
    for p in range(4):
        for q in range(tiles):
            obj[p, q] = ext_ref[p, :, q * LANES:(q + 1) * LANES]
    window = probe_ref.shape[-1]
    modes = probe_ref.shape[1]
    count = where_ref.shape[0]
    lane = lax.broadcasted_iota(jnp.int32, (window, LANES), 1)
    acc[...] = jnp.zeros_like(acc)

    def body(step, carry):
        results = []
        for inner in range(group):
            item = step * group + inner
            row = where_ref[item, 0]
            tile = where_ref[item, 1]
            shift = where_ref[item, 2]
            planes = []
            for p in range(4):
                a = obj[p, tile, pl.ds(row, window), :]
                b = obj[p, tile + 1, pl.ds(row, window), :]
                planes.append(pltpu.roll(jnp.where(lane >= shift, a, b), LANES - shift, 1))
            o1, o2 = (planes[0], planes[2]), (planes[1], planes[3])
            probes = [(probe_ref[0, m], probe_ref[1, m]) for m in range(modes)]
            amp = amp_ref[where_ref[item, 3]].astype(jnp.float32)
            g1, g2 = position_gradient(o1, o2, probes, amp, weight_ref[item], tab)
            results.append((row, tile, shift, (g1[0], g2[0], g1[1], g2[1])))
        for row, tile, shift, grads in results:
            for p in range(4):
                rolled = pltpu.roll(grads[p], shift, 1)
                zero = jnp.zeros_like(rolled)
                here = (p, tile, pl.ds(row, window))
                there = (p, tile + 1, pl.ds(row, window))
                acc[here] = acc[here] + jnp.where(lane >= shift, rolled, zero)
                acc[there] = acc[there] + jnp.where(lane >= shift, zero, rolled)
        return carry

    lax.fori_loop(0, count // group, body, 0)
    for p in range(4):
        for q in range(tiles):
            out_ref[p, :, q * LANES:(q + 1) * LANES] = acc[p, q]


def compute(where, weight, tables, probe_modes, amps, ext):
    vmem = pl.BlockSpec(memory_space=pltpu.VMEM)
    smem = pl.BlockSpec(memory_space=pltpu.SMEM)
    count = where.shape[0]
    group = 2 if count % 2 == 0 else 1
    return pl.pallas_call(
        lambda *refs: compute_kernel(group, *refs),
        out_shape=jax.ShapeDtypeStruct(ext.shape, jnp.float32),
        in_specs=[smem, smem, vmem, vmem, vmem, vmem],
        out_specs=vmem,
        scratch_shapes=[
            pltpu.VMEM((4, ext.shape[2] // LANES, ext.shape[1], LANES), jnp.float32),
            pltpu.VMEM((4, ext.shape[2] // LANES, ext.shape[1], LANES), jnp.float32),
        ],
        compiler_params=pltpu.CompilerParams(vmem_limit_bytes=60 << 20),
        name="positions",
    )(where, weight, tables, probe_modes, amps, ext)


def plan(home_offset, sur_offset, sur_helper, half):
    helper = sur_helper[0, 0]
    columns = lax.axis_size("col")
    my_column = lax.axis_index("col")
    live = helper >= 0
    to_right = live & (helper % columns == (my_column + 1) % columns)
    to_left = live & jnp.logical_not(to_right)
    right_rank = jnp.cumsum(to_right.astype(jnp.int32)) - 1
    left_rank = jnp.cumsum(to_left.astype(jnp.int32)) - 1
    homes = home_offset.shape[3]
    held = jnp.where(to_right, right_rank, half + left_rank)
    held = homes + jnp.where(live, held, 0)
    index = jnp.concatenate([jnp.arange(homes, dtype=jnp.int32), held.astype(jnp.int32)])
    rows = jnp.concatenate([home_offset[0, 0, 0], sur_offset[0, 0, 0]])
    cols = jnp.concatenate([home_offset[0, 0, 1], sur_offset[0, 0, 1]]) + (LANES - MARGIN)
    where = jnp.stack([rows, cols // LANES, cols % LANES, index], axis=1).astype(jnp.int32)
    weight = jnp.concatenate([jnp.ones((homes,), jnp.float32), live.astype(jnp.float32)])
    return where, weight


def shards(object_tiles, probe_modes, home_offset, home_amp, sur_offset, sur_helper, help_amp):
    window = probe_modes.shape[-1]
    tile = object_tiles.shape[-1]
    half = help_amp.shape[2] // 2
    m = MARGIN
    where, weight = plan(home_offset, sur_offset, sur_helper, half)
    amps_right = passed_along(help_amp[0, 0, :half], "col", -1)
    amps_left = passed_along(help_amp[0, 0, half:], "col", 1)
    amps = jnp.concatenate([home_amp[0, 0], amps_right, amps_left], axis=0)
    x = object_tiles.reshape(4, tile, tile)
    up = shift_along(x[:, tile - m:], "row", 1)
    down = shift_along(x[:, :m], "row", -1)
    x = jnp.concatenate([up, x, down], axis=1)
    left = shift_along(x[:, :, tile - m:], "col", 1)
    right = shift_along(x[:, :, :m], "col", -1)
    edge = jnp.zeros(left.shape[:2] + (LANES - m,), jnp.float32)
    ext = jnp.concatenate([edge, left, x, right, edge], axis=2)
    grad = compute(where, weight, jnp.asarray(split_tables(window)), probe_modes, amps, ext)
    to_left = shift_along(grad[:, :, LANES - m:LANES], "col", -1)
    to_right = shift_along(grad[:, :, LANES + tile:LANES + tile + m], "col", 1)
    center = grad[:, :, LANES:LANES + tile]
    center = jnp.concatenate(
        [center[:, :, :m] + to_right, center[:, :, m:tile - m], center[:, :, tile - m:] + to_left],
        axis=2,
    )
    to_up = shift_along(center[:, :m], "row", -1)
    to_down = shift_along(center[:, m + tile:], "row", 1)
    center = center[:, m:m + tile]
    center = jnp.concatenate(
        [center[:, :m] + to_down, center[:, m:tile - m], center[:, tile - m:] + to_up], axis=1
    )
    return center.reshape(object_tiles.shape)


def solution(mesh):
    return jax.shard_map(
        shards,
        mesh=mesh,
        in_specs=(
            P(None, None, "row", "col"),
            P(),
            P("row", "col", None, None),
            P("row", "col", None, None, None),
            P("row", "col", None, None),
            P("row", "col", None),
            P("row", "col", None, None, None),
        ),
        out_specs=P(None, None, "row", "col"),
        check_vma=False,
    )
```

time: 245 us -> 111 us (0.45); the launches traced: 240 us -> 110 us
  matrix products: 87 us -> 0 us
  local copies, waits for them, and re-layouts: 50.8 us -> 17 us
  loops' own time: 23.8 us -> 0 us
  Pallas kernels: 0 us -> 19.3 us
  waiting for transfers between devices: 37.1 us -> 34.2 us
    dot_general x98 -> x0, matrix products: 87 us -> none  [the longest x96 85 us: right_product(): return jnp.matmul(left_side, right_side, precision=lax.Precision.HIGHEST)]
    another operation x3 -> x0, loops' own time: 23.8 us -> none  [the longest x1 23.5 us: add_patches(): return lax.fori_loop(0, grads.shape[0], add_one, total)]
    dynamic_update_slice x6 -> x0, local copies, waits for them, and re-layouts: 20.5 us -> none  [add_one(): lax.dynamic_update_slice(acc, current + piece, (zero, zero, rows_at[item]...]
    pallas_call x0 -> x1, Pallas kernels: none -> 19.3 us  [compute(): pl.pallas_call(lambda *refs: compute_kernel(group, *refs), out_shape=jax....]
    gather x18 -> x0, local copies, waits for them, and re-layouts: 15.9 us -> none
    dynamic_slice x12 -> x0, local copies, waits for them, and re-layouts: 7.05 us -> none  [the longest x6 3.53 us: add_one(): rows_at[item]]
    slice x4 -> x10, local copies, waits for them, and re-layouts: 1.41 us -> 6.02 us  [the longest x1 1.68 us: shards(): center[:, :, m:tile - m]]
    concatenate x1 -> x2, local copies, waits for them, and re-layouts: 0.01 us -> 4.23 us  [the longest x1 4.13 us: shards(): ext = jnp.concatenate([edge, left, x, right, edge], axis=2)]
  transfers between devices with their start and end apart: 10 -> 10, of which waited for: 7 -> 5; matrix products, arithmetic and copies ran while one was open for 3% -> 16% of each run, Pallas kernels for 0% -> 0%
where the time goes in v1:
time: 111 us; the launch traced here: 110 us
  waiting for transfers between devices  34.2 us (31%)
  starting transfers between devices  25.7 us (23%)
  Pallas kernels  19.3 us (17%)
  local copies, waits for them, and re-layouts  17 us (15%)
  other arithmetic  13.5 us (12%)
    ppermute x8, waiting for transfers between devices, shift_along(): return lax.ppermute(block, axis, pairs)  34.2 us
    ppermute x8, starting transfers between devices, shift_along(): return lax.ppermute(block, axis, pairs)  24.2 us
    pallas_call x1, Pallas kernels, compute(): pl.pallas_call(lambda *refs: compute_kernel(group, *refs), out_shape=jax....  19.3 us
    concatenate x1, local copies, waits for them, and re-layouts, shards(): ext = jnp.concatenate([edge, left, x, right, edge], axis=2)  4.13 us
    ppermute x4, local copies, waits for them, and re-layouts, shift_along(): return lax.ppermute(block, axis, pairs)  2.93 us
  transfers between devices with their start and end apart: 10, of which 5 were waited for; matrix products, arithmetic and copies ran while one was open for 16% of the time, Pallas kernels for 0%

profile of v1, /device:TPU:9, one launch (start us, length us, event | category | flops | bytes accessed | tf_op | source)
XLA Modules:
  0.0 110.0 jit_solution(17976551659156595976)
XLA Ops:
  0.0 1.2 %fusion.8 = (f32[4,64,256]{2,1,0:T(8,128)S(1)}, f32[4,64,256]{2,1,0:T(8,128)S(1)}) fusion(f32[4,256,256]{2,1,0:T(8,128)} %bitcast.38), kind=kLoop, calls=%fused_computation.46 | loop fusion | bytes 1048576 | tf_op jit(solution)/shard_map/slice | solution.py:204
  1.2 3.7 %collective-permute-start.2 = (f32[4,64,256]{2,1,0:T(8,128)S(1)}, f32[4,64,256]{2,1,0:T(8,128)S(1)}, u32[]{:S(2)}, u32[]{:S(2)}) collective-permute-start(f32[4,64,256]{2,1,0:T(8,128)S(1)} %get-tuple-element.13), channel_id=1, source_target_pairs={{0,8},{8,16},{16,24},{1,9},{9,17},{17,25},{2,10},{10,18},{18,26},{... | collective-permute-start | bytes 786440 | tf_op jit(solution)/shard_map/ppermute | solution.py:20
  4.9 1.9 %collective-permute-start.3 = (f32[4,64,256]{2,1,0:T(8,128)S(1)}, f32[4,64,256]{2,1,0:T(8,128)S(1)}, u32[]{:S(2)}, u32[]{:S(2)}) collective-permute-start(f32[4,64,256]{2,1,0:T(8,128)S(1)} %get-tuple-element.14), channel_id=1, source_target_pairs={{8,0},{16,8},{24,16},{9,1},{17,9},{25,17},{10,2},{18,10},{26,18},{... | collective-permute-start | bytes 786440 | tf_op jit(solution)/shard_map/ppermute | solution.py:20
  6.8 1.5 %slice_bitcast_fusion.1 = (bf16[2,128,128]{2,1,0:T(8,128)(2,1)}, bf16[2,128,128]{2,1,0:T(8,128)(2,1)}) fusion(bf16[1,1,4,128,128]{4,3,2,1,0:T(8,128)(2,1)} %param.14), kind=kLoop, calls=%fused_computation.11 | loop fusion | bytes 262144 | tf_op jit(solution)/shard_map/squeeze | solution.py:200
  8.3 1.1 %collective-permute-start = (bf16[2,128,128]{2,1,0:T(8,128)(2,1)}, bf16[2,128,128]{2,1,0:T(8,128)(2,1)}, u32[]{:S(2)}, u32[]{:S(2)}) collective-permute-start(bf16[2,128,128]{2,1,0:T(8,128)(2,1)} %get-tuple-element.15), channel_id=1, source_target_pairs={{1,0},{2,1},{3,2},{4,3},{5,4},{6,5},{7,6},{0,7},{9,8},{10,9},{11,1... | collective-permute-start | bytes 196616 | tf_op jit(solution)/shard_map/ppermute | solution.py:25
  9.8 1.2 %bitcast_compare_fusion = pred[4]{0:T(512)(128)(4,1)} fusion(s32[1,1,4]{2,1,0:T(1,128)} %param.13), kind=kLoop, calls=%fused_computation.38 | loop fusion | flops 4 | bytes 20 | tf_op jit(solution)/shard_map/ge | solution.py:178
  12.7 0.8 slice_bitcast_fusion.5
  13.5 1.3 %slice_bitcast_fusion.4 = (s32[4]{0:T(128)}, s32[4,1]{0,1:T(1,128)S(1)}) fusion(s32[1,1,2,4]{3,2,1,0:T(2,128)} %param.12), kind=kLoop, calls=%fused_computation.41 | loop fusion | bytes 64 | tf_op jit(solution)/shard_map/squeeze | solution.py:187
  16.4 4.0 %collective-permute-start.4 = (f32[4,384,64]{1,2,0:T(8,128)S(1)}, f32[4,384,64]{1,2,0:T(8,128)}, u32[]{:S(2)}, u32[]{:S(2)}) collective-permute-start(f32[4,384,64]{1,2,0:T(8,128)S(1)} %copy.16), channel_id=1, source_target_pairs={{0,1},{1,2},{2,3},{3,4},{4,5},{5,6},{6,7},{8,9},{9,10},{10,11},{11... | collective-permute-start | bytes 1179656 | tf_op jit(solution)/shard_map/ppermute | solution.py:20
  20.5 1.0 copy.17
  21.5 2.1 %collective-permute-start.5 = (f32[4,384,64]{1,2,0:T(8,128)}, f32[4,384,64]{1,2,0:T(8,128)S(1)}, u32[]{:S(2)}, u32[]{:S(2)}) collective-permute-start(f32[4,384,64]{1,2,0:T(8,128)} %copy.17), channel_id=1, source_target_pairs={{1,0},{2,1},{3,2},{4,3},{5,4},{6,5},{7,6},{9,8},{10,9},{11,10},{12... | collective-permute-start | bytes 1179656 | tf_op jit(solution)/shard_map/ppermute | solution.py:20
  23.6 0.7 add_bitcast_fusion
  25.2 1.3 %pad_convert_fusion.refs_1_ = f32[6]{0:T(128)} fusion(pred[4]{0:T(512)(128)(4,1)} %bitcast_compare_fusion), kind=kLoop, calls=%fused_computation.26 | loop fusion | flops 6 | bytes 28 | tf_op jit(solution)/shard_map/concatenate | solution.py:190
  26.5 1.6 %pad_maximum_fusion.5.refs_4_ = bf16[6,128,128]{2,1,0:T(8,128)(2,1)} fusion(bf16[2,128,128]{2,1,0:T(8,128)(2,1)} %collective-permute-done.1, bf16[2,128,128]{2,1,0:T(8,128)(2,1)} %collective-permute-done, bf16[2,128,128]{2,1,0:T(8,128)(2,1)} %bitcast.40), kind=kLoop, calls=%fused_computation.9 | loop fusion | flops 196608 | bytes 393216 | tf_op jit(solution)/shard_map/concatenate | solution.py:202
  28.1 8.9 %collective-permute-done.4 = f32[4,384,64]{1,2,0:T(8,128)} collective-permute-done((f32[4,384,64]{1,2,0:T(8,128)S(1)}, f32[4,384,64]{1,2,0:T(8,128)}, u32[]{:S(2)}, u32[]{:S(2)}) %collective-permute-start.4) | collective-permute-done | bytes 393248 | tf_op jit(solution)/shard_map/ppermute | solution.py:20
  36.9 1.3 %copy.18 = f32[4,384,64]{2,1,0:T(8,128)S(1)} copy(f32[4,384,64]{1,2,0:T(8,128)} %collective-permute-done.4) | data formatting | bytes 786432 | tf_op jit(solution)/shard_map/ppermute | solution.py:20
  38.2 1.2 %copy.19 = f32[4,384,64]{2,1,0:T(8,128)} copy(f32[4,384,64]{1,2,0:T(8,128)S(1)} %collective-permute-done.5) | data formatting | bytes 786432 | tf_op jit(solution)/shard_map/ppermute | solution.py:20
  39.4 4.1 %concatenate.53.refs_5_ = f32[4,384,512]{2,1,0:T(8,128)} concatenate(f32[4,384,64]{2,1,0:T(8,128)S(1)} %broadcast_in_dim.5, f32[4,384,64]{2,1,0:T(8,128)S(1)} %copy.18, f32[4,384,256]{2,1,0:T(8,128)S(1)} %pad_maximum_fusion, f32[4,384,64]{2,1,0:T(8,128)} %copy.19, f32[4,384,64]{2,1,0:T(8,128)S(1)} %broadcast_in_dim.5), dimensions={2} | concatenate | bytes 6291456 | tf_op jit(solution)/shard_map/concatenate | solution.py:210
  43.6 19.3 %positions.1 = f32[4,384,512]{2,1,0:T(8,128)} custom-call(s32[6,4]{1,0:T(8,128)} %pad_add_fusion.refs_0_, f32[6]{0:T(128)} %pad_convert_fusion.refs_1_, bf16[2,6,128,128]{3,2,1,0:T(8,128)(2,1)} %constant.75.clone.refs_2_, f32[2,2,128,128]{3,2,1,0:T(8,128)} %refs_3_.1, bf16[6,128,128]{2,1,0:T(8,128)(2,1)} %pad_maximum_fusion.5.refs_4_, ...), custom_call_target="tpu_custom_call" | custom-call | tf_op jit(solution)/shard_map/positions/pallas_call | solution.py:160
  62.8 1.1 %slice-done = f32[4,384,64]{2,1,0:T(8,128)S(1)} async-done(((f32[4,384,512]{2,1,0:T(8,128)}), f32[4,384,64]{2,1,0:T(8,128)S(1)}, s32[]{:S(2)}) %slice-start) | async-done | bytes 393240 | tf_op jit(solution)/shard_map/slice | solution.py:213
  64.2 3.9 %collective-permute-start.6 = (f32[4,384,64]{1,2,0:T(8,128)S(1)}, f32[4,384,64]{1,2,0:T(8,128)S(1)}, u32[]{:S(2)}, u32[]{:S(2)}) collective-permute-start(f32[4,384,64]{1,2,0:T(8,128)S(1)} %copy.20), channel_id=1, source_target_pairs={{0,1},{1,2},{2,3},{3,4},{4,5},{5,6},{6,7},{8,9},{9,10},{10,11},{11... | collective-permute-start | bytes 1179656 | tf_op jit(solution)/shard_map/ppermute | solution.py:20
  68.1 9.5 %collective-permute-done.6 = f32[4,384,64]{1,2,0:T(8,128)S(1)} collective-permute-done((f32[4,384,64]{1,2,0:T(8,128)S(1)}, f32[4,384,64]{1,2,0:T(8,128)S(1)}, u32[]{:S(2)}, u32[]{:S(2)}) %collective-permute-start.6) | collective-permute-done | bytes 393248 | tf_op jit(solution)/shard_map/ppermute | solution.py:20
  77.9 1.7 %slice_add_fusion.1 = (f32[4,384,64]{2,1,0:T(8,128)S(1)}, f32[4,384,64]{2,1,0:T(8,128)S(1)}) fusion(f32[4,384,64]{2,1,0:T(8,128)S(1)} %copy.21, f32[4,384,512]{2,1,0:T(8,128)} %positions.1), kind=kLoop, calls=%fused_computation.4 | loop fusion | flops 98304 | bytes 1966080 | tf_op jit(solution)/shard_map/add | solution.py:216
  79.8 3.2 %collective-permute-start.7 = (f32[4,384,64]{1,2,0:T(8,128)S(1)}, f32[4,384,64]{1,2,0:T(8,128)S(1)}, u32[]{:S(2)}, u32[]{:S(2)}) collective-permute-start(f32[4,384,64]{1,2,0:T(8,128)S(1)} %copy.22), channel_id=1, source_target_pairs={{1,0},{2,1},{3,2},{4,3},{5,4},{6,5},{7,6},{9,8},{10,9},{11,10},{12... | collective-permute-start | bytes 1179656 | tf_op jit(solution)/shard_map/ppermute | solution.py:20
  83.0 1.7 %slice.94 = f32[4,384,128]{2,1,0:T(8,128)S(1)} slice(f32[4,384,512]{2,1,0:T(8,128)} %positions.1), slice={[0:4], [0:384], [192:320]} | slice | bytes 1572864 | tf_op jit(solution)/shard_map/slice | solution.py:216
  84.7 6.8 %collective-permute-done.7 = f32[4,384,64]{1,2,0:T(8,128)S(1)} collective-permute-done((f32[4,384,64]{1,2,0:T(8,128)S(1)}, f32[4,384,64]{1,2,0:T(8,128)S(1)}, u32[]{:S(2)}, u32[]{:S(2)}) %collective-permute-start.7) | collective-permute-done | bytes 393248 | tf_op jit(solution)/shard_map/ppermute | solution.py:20
  91.7 1.4 %slice_add_fusion = f32[4,384,64]{2,1,0:T(8,128)S(1)} fusion(f32[4,384,64]{2,1,0:T(8,128)S(1)} %copy.23, f32[4,384,512]{2,1,0:T(8,128)} %positions.1), kind=kLoop, calls=%fused_computation.3 | loop fusion | flops 98304 | bytes 1179648 | tf_op jit(solution)/shard_map/add | solution.py:216
  93.3 3.4 %collective-permute-start.8 = (f32[4,64,256]{2,1,0:T(8,128)S(1)}, f32[4,64,256]{2,1,0:T(8,128)S(1)}, u32[]{:S(2)}, u32[]{:S(2)}) collective-permute-start(f32[4,64,256]{2,1,0:T(8,128)S(1)} %pad_maximum_fusion.4), channel_id=1, source_target_pairs={{0,8},{8,16},{16,24},{1,9},{9,17},{17,25},{2,10},{10,18},{18,26},{... | collective-permute-start | bytes 786440 | tf_op jit(solution)/shard_map/ppermute | solution.py:20
  96.7 3.3 %collective-permute-done.8 = f32[4,64,256]{2,1,0:T(8,128)S(1)} collective-permute-done((f32[4,64,256]{2,1,0:T(8,128)S(1)}, f32[4,64,256]{2,1,0:T(8,128)S(1)}, u32[]{:S(2)}, u32[]{:S(2)}) %collective-permute-start.8) | collective-permute-done | bytes 262176 | tf_op jit(solution)/shard_map/ppermute | solution.py:20
  100.3 1.9 %collective-permute-start.9 = (f32[4,64,256]{2,1,0:T(8,128)S(1)}, f32[4,64,256]{2,1,0:T(8,128)S(1)}, u32[]{:S(2)}, u32[]{:S(2)}) collective-permute-start(f32[4,64,256]{2,1,0:T(8,128)S(1)} %get-tuple-element.10), channel_id=1, source_target_pairs={{8,0},{16,8},{24,16},{9,1},{17,9},{25,17},{10,2},{18,10},{26,18},{... | collective-permute-start | bytes 786440 | tf_op jit(solution)/shard_map/ppermute | solution.py:20
  103.0 5.8 %collective-permute-done.9 = f32[4,64,256]{2,1,0:T(8,128)S(1)} collective-permute-done((f32[4,64,256]{2,1,0:T(8,128)S(1)}, f32[4,64,256]{2,1,0:T(8,128)S(1)}, u32[]{:S(2)}, u32[]{:S(2)}) %collective-permute-start.9) | collective-permute-done | bytes 262176 | tf_op jit(solution)/shard_map/ppermute | solution.py:20
  108.9 1.0 pad_maximum_fusion.2
  (35 shorter events, 6.8 us)
Async XLA Ops:
  0.0 15.8 %copy-start = (f32[2,2,256,256]{3,2,1,0:T(8,128)S(1)}, f32[2,2,256,256]{3,2,1,0:T(8,128)}, u32[]{:S(2)}) copy-start(f32[2,2,256,256]{3,2,1,0:T(8,128)} %param.8) | copy-start | bytes 3145732
  1.2 14.6 %collective-permute-start.2 = (f32[4,64,256]{2,1,0:T(8,128)S(1)}, f32[4,64,256]{2,1,0:T(8,128)S(1)}, u32[]{:S(2)}, u32[]{:S(2)}) collective-permute-start(f32[4,64,256]{2,1,0:T(8,128)S(1)} %get-tuple-element.13), channel_id=1, source_target_pairs={{0,8},{8,16},{16,24},{1,9},{9,17},{17,25},{2,10},{10,18},{18,26},{... | collective-permute-start | bytes 786440 | tf_op jit(solution)/shard_map/ppermute | solution.py:20
  4.9 10.9 %collective-permute-start.3 = (f32[4,64,256]{2,1,0:T(8,128)S(1)}, f32[4,64,256]{2,1,0:T(8,128)S(1)}, u32[]{:S(2)}, u32[]{:S(2)}) collective-permute-start(f32[4,64,256]{2,1,0:T(8,128)S(1)} %get-tuple-element.14), channel_id=1, source_target_pairs={{8,0},{16,8},{24,16},{9,1},{17,9},{25,17},{10,2},{18,10},{26,18},{... | collective-permute-start | bytes 786440 | tf_op jit(solution)/shard_map/ppermute | solution.py:20
  8.3 18.1 %collective-permute-start = (bf16[2,128,128]{2,1,0:T(8,128)(2,1)}, bf16[2,128,128]{2,1,0:T(8,128)(2,1)}, u32[]{:S(2)}, u32[]{:S(2)}) collective-permute-start(bf16[2,128,128]{2,1,0:T(8,128)(2,1)} %get-tuple-element.15), channel_id=1, source_target_pairs={{1,0},{2,1},{3,2},{4,3},{5,4},{6,5},{7,6},{0,7},{9,8},{10,9},{11,1... | collective-permute-start | bytes 196616 | tf_op jit(solution)/shard_map/ppermute | solution.py:25
  9.5 17.0 %collective-permute-start.1 = (bf16[2,128,128]{2,1,0:T(8,128)(2,1)}, bf16[2,128,128]{2,1,0:T(8,128)(2,1)}, u32[]{:S(2)}, u32[]{:S(2)}) collective-permute-start(bf16[2,128,128]{2,1,0:T(8,128)(2,1)} %get-tuple-element.16), channel_id=1, source_target_pairs={{7,0},{0,1},{1,2},{2,3},{3,4},{4,5},{5,6},{6,7},{15,8},{8,9},{9,10... | collective-permute-start | bytes 196616 | tf_op jit(solution)/shard_map/ppermute | solution.py:25
  16.4 20.5 %collective-permute-start.4 = (f32[4,384,64]{1,2,0:T(8,128)S(1)}, f32[4,384,64]{1,2,0:T(8,128)}, u32[]{:S(2)}, u32[]{:S(2)}) collective-permute-start(f32[4,384,64]{1,2,0:T(8,128)S(1)} %copy.16), channel_id=1, source_target_pairs={{0,1},{1,2},{2,3},{3,4},{4,5},{5,6},{6,7},{8,9},{9,10},{10,11},{11... | collective-permute-start | bytes 1179656 | tf_op jit(solution)/shard_map/ppermute | solution.py:20
  21.5 16.7 %collective-permute-start.5 = (f32[4,384,64]{1,2,0:T(8,128)}, f32[4,384,64]{1,2,0:T(8,128)S(1)}, u32[]{:S(2)}, u32[]{:S(2)}) collective-permute-start(f32[4,384,64]{1,2,0:T(8,128)} %copy.17), channel_id=1, source_target_pairs={{1,0},{2,1},{3,2},{4,3},{5,4},{6,5},{7,6},{9,8},{10,9},{11,10},{12... | collective-permute-start | bytes 1179656 | tf_op jit(solution)/shard_map/ppermute | solution.py:20
  62.8 1.1 %slice-start = ((f32[4,384,512]{2,1,0:T(8,128)}), f32[4,384,64]{2,1,0:T(8,128)S(1)}, s32[]{:S(2)}) async-start(f32[4,384,512]{2,1,0:T(8,128)} %positions.1), calls=%async_computation | async-start | bytes 1572864 | tf_op jit(solution)/shard_map/slice | solution.py:213
  64.2 13.4 %collective-permute-start.6 = (f32[4,384,64]{1,2,0:T(8,128)S(1)}, f32[4,384,64]{1,2,0:T(8,128)S(1)}, u32[]{:S(2)}, u32[]{:S(2)}) collective-permute-start(f32[4,384,64]{1,2,0:T(8,128)S(1)} %copy.20), channel_id=1, source_target_pairs={{0,1},{1,2},{2,3},{3,4},{4,5},{5,6},{6,7},{8,9},{9,10},{10,11},{11... | collective-permute-start | bytes 1179656 | tf_op jit(solution)/shard_map/ppermute | solution.py:20
  79.8 11.7 %collective-permute-start.7 = (f32[4,384,64]{1,2,0:T(8,128)S(1)}, f32[4,384,64]{1,2,0:T(8,128)S(1)}, u32[]{:S(2)}, u32[]{:S(2)}) collective-permute-start(f32[4,384,64]{1,2,0:T(8,128)S(1)} %copy.22), channel_id=1, source_target_pairs={{1,0},{2,1},{3,2},{4,3},{5,4},{6,5},{7,6},{9,8},{10,9},{11,10},{12... | collective-permute-start | bytes 1179656 | tf_op jit(solution)/shard_map/ppermute | solution.py:20
  93.3 6.7 %collective-permute-start.8 = (f32[4,64,256]{2,1,0:T(8,128)S(1)}, f32[4,64,256]{2,1,0:T(8,128)S(1)}, u32[]{:S(2)}, u32[]{:S(2)}) collective-permute-start(f32[4,64,256]{2,1,0:T(8,128)S(1)} %pad_maximum_fusion.4), channel_id=1, source_target_pairs={{0,8},{8,16},{16,24},{1,9},{9,17},{17,25},{2,10},{10,18},{18,26},{... | collective-permute-start | bytes 786440 | tf_op jit(solution)/shard_map/ppermute | solution.py:20
  100.3 8.4 %collective-permute-start.9 = (f32[4,64,256]{2,1,0:T(8,128)S(1)}, f32[4,64,256]{2,1,0:T(8,128)S(1)}, u32[]{:S(2)}, u32[]{:S(2)}) collective-permute-start(f32[4,64,256]{2,1,0:T(8,128)S(1)} %get-tuple-element.10), channel_id=1, source_target_pairs={{8,0},{16,8},{24,16},{9,1},{17,9},{25,17},{10,2},{18,10},{26,18},{... | collective-permute-start | bytes 786440 | tf_op jit(solution)/shard_map/ppermute | solution.py:20

commit v2 on v1

v2 whole, which is shorter than its diff:
```python
import functools
import math

import numpy as np
import ml_dtypes
import jax
import jax.numpy as jnp
from jax import lax
from jax.experimental import pallas as pl
from jax.experimental.pallas import tpu as pltpu
from jax.sharding import PartitionSpec as P

MARGIN = 64
LANES = 128
EPS = 0.1
MESH = pl.DeviceIdType.MESH
SIDES = ((1, 0), (-1, 0), (0, 1), (0, -1), (1, 1), (-1, 1), (1, -1), (-1, -1))


def split_tables(window):
    index = np.arange(window)
    spectral = np.exp(-2j * np.pi / window * (index[:, None] * index[None, :] % window))
    spectral /= math.sqrt(window)
    freq = np.where(index >= window // 2, index - window, index).astype(np.float64)
    carrier = np.exp(-1j * np.pi / window * freq**2)
    propagate = np.conj(spectral) @ (carrier[:, None] * spectral)
    blocks = []
    for table in (propagate, spectral):
        blocks += [table.real, table.imag, -table.imag]
    full = np.stack(blocks).astype(np.float32)
    high = full.astype(ml_dtypes.bfloat16)
    low = (full - high.astype(np.float32)).astype(ml_dtypes.bfloat16)
    return np.stack([high, low])


def split(x):
    high = x.astype(jnp.bfloat16)
    low = (x - high.astype(jnp.float32)).astype(jnp.bfloat16)
    return high, low


def square(tab, which, flip):
    def one(part):
        re, im, neg = (tab[part, 3 * which + k] for k in range(3))
        if flip:
            im, neg = neg, im
        top = jnp.concatenate([re, im], axis=1)
        return jnp.concatenate([top, jnp.concatenate([neg, re], axis=1)], axis=0)

    return one(0), one(1)


def dot(a, b):
    return jnp.dot(a, b, preferred_element_type=jnp.float32)


def sandwich(fields, tab, which, conj):
    rows = [jnp.concatenate([re, im], axis=1) for re, im in fields]
    high, low = split(jnp.concatenate(rows, axis=0))
    t_high, t_low = square(tab, which, conj)
    first = dot(
        jnp.concatenate([high, low, high], axis=1),
        jnp.concatenate([t_high, t_high, t_low], axis=0),
    )
    w = first.shape[1] // 2
    count = len(fields)
    top = jnp.concatenate([first[m * w:(m + 1) * w, :w] for m in range(count)], axis=1)
    low_half = jnp.concatenate([first[m * w:(m + 1) * w, w:] for m in range(count)], axis=1)
    high, low = split(jnp.concatenate([top, low_half], axis=0))
    t_high, t_low = square(tab, which, not conj)
    second = dot(
        jnp.concatenate([t_high, t_low, t_high], axis=1),
        jnp.concatenate([high, high, low], axis=0),
    )
    return [
        (second[:w, m * w:(m + 1) * w], second[w:, m * w:(m + 1) * w]) for m in range(count)
    ]


def times(a, b):
    return a[0] * b[0] - a[1] * b[1], a[0] * b[1] + a[1] * b[0]


def conj_times(a, b):
    return a[0] * b[0] + a[1] * b[1], a[0] * b[1] - a[1] * b[0]


def lanes(shape):
    return lax.broadcasted_iota(jnp.int32, shape, len(shape) - 1)


def pair_up(re, im, keep_high):
    half = LANES // 2
    if keep_high:
        return jnp.where(lanes(re.shape) < half, pltpu.roll(re, half, 1), im)
    return jnp.where(lanes(re.shape) < half, re, pltpu.roll(im, half, 1))


def kernel(
    grid_shape, home_off, sur_off, helper_ref, tab, probe_ref, x_ref, home_amp, help_amp, out_ref,
    meta, obj0, obj1, acc, pack, side, gpack, grow, gside, gcorner, amps, waves, patches,
    send_sem, recv_sem, amp_send, amp_recv,
):
    n_row, n_col = grid_shape
    obj = (obj0, obj1)
    row, col = lax.axis_index("row"), lax.axis_index("col")
    tile = x_ref.shape[2]
    window = probe_ref.shape[-1]
    modes = probe_ref.shape[1]
    homes = home_amp.shape[0]
    slots = help_amp.shape[0]
    half = slots // 2
    count = homes + slots
    m = MARGIN
    ext = tile + 2 * m
    tiles = obj0.shape[1]
    inner = tile // LANES

    def inside(dr, dc):
        r, c = row + dr, col + dc
        return (r >= 0) & (r < n_row) & (c >= 0) & (c < n_col)

    ring = [(row, lax.rem(col + 1, n_col)), (row, lax.rem(col + n_col - 1, n_col))]
    barrier = pltpu.get_barrier_semaphore()
    for target in ring:
        pl.semaphore_signal(barrier, inc=1, device_id=target, device_id_type=MESH)
    for dr, dc in SIDES:
        if dr != 0:
            @pl.when(inside(dr, dc))
            def _(dr=dr, dc=dc):
                pl.semaphore_signal(
                    barrier, inc=1, device_id=(row + dr, col + dc), device_id_type=MESH
                )

    for k in range(2):
        first, last = x_ref[:, k, :, 0:LANES], x_ref[:, k, :, tile - LANES:tile]
        pack[k, 0] = pair_up(first[0], first[1], False)
        pack[k, 1] = pair_up(last[0], last[1], True)

    vertical = jnp.where(row > 0, 1, 0) + jnp.where(row + 1 < n_row, 1, 0)
    across = 1 + jnp.where(col > 0, 1, 0) + jnp.where(col + 1 < n_col, 1, 0)
    pl.semaphore_wait(barrier, 2 + vertical * across)

    def remote(src, dst, phase, k, index, target):
        return pltpu.make_async_remote_copy(
            src_ref=src, dst_ref=dst,
            send_sem=send_sem.at[phase, k, index], recv_sem=recv_sem.at[phase, k, index],
            device_id=target, device_id_type=MESH,
        )

    def edge(d, source):
        if d == 0:
            return slice(m, m + tile) if source == "ext" else slice(0, tile)
        if source == "ext":
            return slice(ext - m, ext) if d > 0 else slice(0, m)
        return slice(tile - m, tile) if d > 0 else slice(0, m)

    def halo_copies(n, k):
        dr, dc = SIDES[n]
        target = (row + dr, col + dc)
        landing = edge(-dr, "ext")
        if dc == 0:
            return [
                remote(
                    x_ref.at[:, k, edge(dr, "tile"), q * LANES:(q + 1) * LANES],
                    obj[k].at[:, 1 + q, landing, :], 0, k, n + 8 * q, target,
                )
                for q in range(inner)
            ]
        s = 1 if dc > 0 else 0
        return [remote(pack.at[k, s, edge(dr, "tile")], side.at[k, 1 - s, landing], 0, k, n, target)]

    def grad_copies(n, k):
        dr, dc = SIDES[n]
        target = (row + dr, col + dc)
        take = edge(dr, "ext")
        if dc == 0:
            u = 1 if dr > 0 else 0
            return [remote(acc.at[:, k, 1:1 + inner, take, :], grow.at[k, 1 - u], 1, k, n, target)]
        s = 1 if dc > 0 else 0
        source = gpack.at[k, s, take]
        if dr == 0:
            return [remote(source, gside.at[k, 1 - s], 1, k, n, target)]
        u = 1 if dr > 0 else 0
        return [remote(source, gcorner.at[k, 1 - s, 1 - u], 1, k, n, target)]

    def start(copies, k):
        for n, (dr, dc) in sorted(enumerate(SIDES), key=lambda e: e[1][1] == 0):
            @pl.when(inside(dr, dc))
            def _(n=n):
                for copy in copies(n, k):
                    copy.start()

    def wait_recv(copies, k):
        for n, (dr, dc) in enumerate(SIDES):
            @pl.when(inside(-dr, -dc))
            def _(n=n):
                for copy in copies(n, k):
                    copy.wait_recv()

    def wait_send(copies, k):
        for n, (dr, dc) in enumerate(SIDES):
            @pl.when(inside(dr, dc))
            def _(n=n):
                for copy in copies(n, k):
                    copy.wait_send()

    start(halo_copies, 0)
    start(halo_copies, 1)
    amp_copies = [
        pltpu.make_async_remote_copy(
            src_ref=help_amp.at[h * half:(h + 1) * half],
            dst_ref=amps.at[homes + h * half:homes + (h + 1) * half],
            send_sem=amp_send.at[h], recv_sem=amp_recv.at[h],
            device_id=ring[1 - h], device_id_type=MESH,
        )
        for h in range(2)
    ]
    for copy in amp_copies:
        copy.start()

    for n, (dr, dc) in enumerate(SIDES):
        @pl.when(jnp.logical_not(inside(-dr, -dc)))
        def _(dr=dr, dc=dc):
            landing = edge(-dr, "ext")
            u = 1 if dr > 0 else 0
            s = 1 if dc > 0 else 0
            for k in range(2):
                if dc == 0:
                    halo = obj[k][:, 1:1 + inner, landing, :]
                    obj[k][:, 1:1 + inner, landing, :] = jnp.zeros(halo.shape, jnp.float32)
                    grow[k, 1 - u] = jnp.zeros(grow.shape[2:], jnp.float32)
                else:
                    rows_here = landing.stop - landing.start
                    side[k, 1 - s, landing] = jnp.zeros((rows_here, LANES), jnp.float32)
                    if dr == 0:
                        gside[k, 1 - s] = jnp.zeros(gside.shape[2:], jnp.float32)
                    else:
                        gcorner[k, 1 - s, 1 - u] = jnp.zeros(gcorner.shape[3:], jnp.float32)

    for h in range(homes):
        c = home_off[1, h] + (LANES - m)
        for at, value in enumerate((home_off[0, h], lax.div(c, LANES), lax.rem(c, LANES), h, 1)):
            meta[h, at] = jnp.int32(value)
    next_column = lax.rem(col + 1, n_col)
    rights, lefts = jnp.int32(0), jnp.int32(0)
    for h in range(slots):
        helper = helper_ref[h]
        live = jnp.where(helper >= 0, 1, 0)
        right = jnp.where(lax.rem(jnp.maximum(helper, 0), n_col) == next_column, live, 0)
        left = live - right
        held = jnp.minimum(right * rights + left * (half + lefts), slots - 1)
        rights, lefts = rights + right, lefts + left
        c = sur_off[1, h] + (LANES - m)
        values = (sur_off[0, h], lax.div(c, LANES), lax.rem(c, LANES), homes + held, live)
        for at, value in enumerate(values):
            meta[homes + h, at] = value

    for a in range(2):
        for k in range(2):
            for q in range(inner):
                obj[k][a, 1 + q, m:m + tile, :] = x_ref[a, k, :, q * LANES:(q + 1) * LANES]
    amps[0:homes] = home_amp[...]
    patches[...] = jnp.zeros_like(patches)

    def unpack(k):
        wait_recv(halo_copies, k)
        lower, upper = side[k, 0], side[k, 1]
        obj[k][0, 0] = pltpu.roll(lower, LANES // 2, 1)
        obj[k][1, 0] = lower
        obj[k][0, tiles - 1] = upper
        obj[k][1, tiles - 1] = pltpu.roll(upper, LANES // 2, 1)

    lane = lanes((window, LANES))

    def cut(item, k):
        at, q, shift = meta[item, 0], meta[item, 1], meta[item, 2]
        out = []
        for a in range(2):
            here = obj[k][a, q, pl.ds(at, window), :]
            there = obj[k][a, q + 1, pl.ds(at, window), :]
            out.append(pltpu.roll(jnp.where(lane >= shift, here, there), LANES - shift, 1))
        return tuple(out)

    def put(item, grad):
        shift = meta[item, 2]
        for a in range(2):
            patches[item, a, tile:tile + window, :] = pltpu.roll(grad[a], shift, 1)

    def total(parts):
        return sum(p[0] for p in parts), sum(p[1] for p in parts)

    probes = lambda: [(probe_ref[0, j], probe_ref[1, j]) for j in range(modes)]
    kept = lambda item: [(waves[item, j, 0], waves[item, j, 1]) for j in range(modes)]

    def keep(item, fields):
        for j, (re, im) in enumerate(fields):
            waves[item, j, 0] = re
            waves[item, j, 1] = im

    def each(fn):
        def step(i, carry):
            for j in range(GROUP):
                fn(i * GROUP + j)
            return carry

        lax.fori_loop(0, count // GROUP, step, 0)

    def enter(item):
        o1 = cut(item, 0)
        keep(item, sandwich([times(p, o1) for p in probes()], tab, 0, False))

    def middle(item):
        o2 = cut(item, 1)
        fields = kept(item)
        far = sandwich([times(b, o2) for b in fields], tab, 1, False)
        intensity = sum(re * re + im * im for re, im in far)
        amp = amps[meta[item, 3]].astype(jnp.float32)
        weight = 2.0 * meta[item, 4].astype(jnp.float32)
        factor = weight * (1.0 - amp * lax.rsqrt(intensity + EPS))
        exits = sandwich([(re * factor, im * factor) for re, im in far], tab, 1, True)
        put(item, total([conj_times(b, e) for b, e in zip(fields, exits)]))
        keep(item, [conj_times(o2, e) for e in exits])

    def leave(item):
        entry = sandwich(kept(item), tab, 0, True)
        put(item, total([conj_times(p, e) for p, e in zip(probes(), entry)]))

    chunk = 32

    def gather(k):
        lane8 = lanes((chunk, LANES))

        def step(i, carry):
            begin = pl.multiple_of(i * chunk, chunk)
            for a in range(2):
                sums = [jnp.zeros((chunk, LANES), jnp.float32) for _ in range(tiles)]
                for item in range(count):
                    at, q, shift = meta[item, 0], meta[item, 1], meta[item, 2]
                    piece = patches[item, a, pl.ds(tile - at + begin, chunk), :]
                    high = jnp.where(lane8 >= shift, piece, 0.0)
                    low = piece - high
                    for t in range(tiles):
                        hit = jnp.where(q == t, 1.0, 0.0)
                        miss = jnp.where(q + 1 == t, 1.0, 0.0)
                        sums[t] = sums[t] + (high * hit + low * miss)
                for t in range(tiles):
                    acc[a, k, t, pl.ds(begin, chunk), :] = sums[t]
            return carry

        lax.fori_loop(0, ext // chunk, step, 0)
        gpack[k, 0] = pair_up(acc[0, k, 0], acc[1, k, 0], True)
        gpack[k, 1] = pair_up(acc[0, k, tiles - 1], acc[1, k, tiles - 1], False)
        start(grad_copies, k)

    def finish(k):
        wait_recv(grad_copies, k)
        low = lanes((tile, LANES)) < LANES // 2
        for q in range(inner):
            for a in range(2):
                value = acc[a, k, 1 + q, m:m + tile, :]
                top = value[:m] + grow[k, 0, a, q]
                bottom = value[tile - m:] + grow[k, 1, a, q]
                value = jnp.concatenate([top, value[m:tile - m], bottom], axis=0)
                for s in range(2):
                    if (s == 0 and q != 0) or (s == 1 and q != inner - 1):
                        continue
                    extra = gside[k, s]
                    extra = jnp.concatenate(
                        [
                            extra[:m] + gcorner[k, s, 0],
                            extra[m:tile - m],
                            extra[tile - m:] + gcorner[k, s, 1],
                        ],
                        axis=0,
                    )
                    if a != s:
                        extra = pltpu.roll(extra, LANES // 2, 1)
                    value = value + jnp.where(low if s == 0 else jnp.logical_not(low), extra, 0.0)
                out_ref[a, k, :, q * LANES:(q + 1) * LANES] = value

    unpack(0)
    each(enter)
    unpack(1)
    for copy in amp_copies:
        copy.wait_recv()
    each(middle)
    gather(1)
    each(leave)
    gather(0)
    finish(1)
    finish(0)
    for k in range(2):
        wait_send(halo_copies, k)
        wait_send(grad_copies, k)
    for copy in amp_copies:
        copy.wait_send()


GROUP = 2


def shards(object_tiles, probe_modes, home_offset, home_amp, sur_offset, sur_helper, help_amp):
    window = probe_modes.shape[-1]
    modes = probe_modes.shape[1]
    tile = object_tiles.shape[-1]
    ext = tile + 2 * MARGIN
    tiles = tile // LANES + 2
    inner = tile // LANES
    count = home_amp.shape[2] + help_amp.shape[2]
    grid_shape = (lax.axis_size("row"), lax.axis_size("col"))
    vmem = pl.BlockSpec(memory_space=pltpu.VMEM)
    smem = pl.BlockSpec(memory_space=pltpu.SMEM)
    f32 = jnp.float32
    return pl.pallas_call(
        functools.partial(kernel, grid_shape),
        out_shape=jax.ShapeDtypeStruct(object_tiles.shape, f32),
        in_specs=[smem] * 3 + [vmem] * 5,
        out_specs=vmem,
        scratch_shapes=[
            pltpu.SMEM((count, 5), jnp.int32),
            pltpu.VMEM((2, tiles, ext, LANES), f32),
            pltpu.VMEM((2, tiles, ext, LANES), f32),
            pltpu.VMEM((2, 2, tiles, ext, LANES), f32),
            pltpu.VMEM((2, 2, tile, LANES), f32),
            pltpu.VMEM((2, 2, ext, LANES), f32),
            pltpu.VMEM((2, 2, ext, LANES), f32),
            pltpu.VMEM((2, 2, 2, inner, MARGIN, LANES), f32),
            pltpu.VMEM((2, 2, tile, LANES), f32),
            pltpu.VMEM((2, 2, 2, MARGIN, LANES), f32),
            pltpu.VMEM((count, window, window), jnp.bfloat16),
            pltpu.VMEM((count, modes, 2, window, window), f32),
            pltpu.VMEM((count, 2, 2 * tile + window, LANES), f32),
            pltpu.SemaphoreType.DMA((2, 2, 8 + 8 * (inner - 1))),
            pltpu.SemaphoreType.DMA((2, 2, 8 + 8 * (inner - 1))),
            pltpu.SemaphoreType.DMA((2,)),
            pltpu.SemaphoreType.DMA((2,)),
        ],
        compiler_params=pltpu.CompilerParams(
            collective_id=0, has_side_effects=True, vmem_limit_bytes=60 << 20
        ),
        name="multislice",
    )(
        home_offset[0, 0], sur_offset[0, 0], sur_helper[0, 0],
        jnp.asarray(split_tables(window)), probe_modes, object_tiles, home_amp[0, 0], help_amp[0, 0],
    )


def solution(mesh):
    return jax.shard_map(
        shards,
        mesh=mesh,
        in_specs=(
            P(None, None, "row", "col"),
            P(),
            P("row", "col", None, None),
            P("row", "col", None, None, None),
            P("row", "col", None, None),
            P("row", "col", None),
            P("row", "col", None, None, None),
        ),
        out_specs=P(None, None, "row", "col"),
        check_vma=False,
    )
```

time: 111 us -> 54.9 us (0.49)
  waiting for transfers between devices: 34.2 us -> 0 us
  Pallas kernels: 19.3 us -> 52.2 us
  starting transfers between devices: 25.7 us -> 0 us
  local copies, waits for them, and re-layouts: 17 us -> 2.29 us
  other arithmetic: 13.5 us -> 0 us
    ppermute x10 -> x0, waiting for transfers between devices: 34.2 us -> none  [the longest x8 34.2 us: shift_along(): return lax.ppermute(block, axis, pairs)]
    pallas_call x1, Pallas kernels: 19.3 us -> 52.2 us  [shards(): pl.pallas_call(functools.partial(kernel, grid_shape), out_shape=jax.Shape...]
    ppermute x10 -> x0, starting transfers between devices: 25.7 us -> none  [the longest x8 24.2 us: shift_along(): return lax.ppermute(block, axis, pairs)]
    slice x10 -> x0, local copies, waits for them, and re-layouts: 6.02 us -> none  [the longest x1 1.68 us: shards(): center[:, :, m:tile - m]]
    concatenate x6 -> x0, other arithmetic: 4.78 us -> none  [the longest x1 1.61 us: shards(): amps = jnp.concatenate([home_amp[0, 0], amps_right, amps_left], axis=0)]
    concatenate x2 -> x0, local copies, waits for them, and re-layouts: 4.23 us -> none  [the longest x1 4.13 us: shards(): ext = jnp.concatenate([edge, left, x, right, edge], axis=2)]
    add x5 -> x0, other arithmetic: 4.18 us -> none  [the longest x1 1.66 us: shards(): center[:, :, :m] + to_right]
    squeeze x3 -> x0, local copies, waits for them, and re-layouts: 3.63 us -> none  [the longest x2 2.08 us: plan(): rows = jnp.concatenate([home_offset[0, 0, 0], sur_offset[0, 0, 0]])]
  transfers between devices with their start and end apart: 10 -> 0, of which waited for: 5 -> 0; matrix products, arithmetic and copies ran while one was open for 16% -> 0% of each run, Pallas kernels for 0% -> 0%
where the time goes in v2:
time: 54.9 us; the launch traced here: 54.5 us
  Pallas kernels  52.2 us (95%)
  local copies, waits for them, and re-layouts  2.29 us (4%)
    pallas_call x1, Pallas kernels, shards(): pl.pallas_call(functools.partial(kernel, grid_shape), out_shape=jax.Shape...  52.2 us
    unnamed x1, local copies, waits for them, and re-layouts  2.29 us

profile of v2, /device:TPU:9, one launch (start us, length us, event | category | flops | bytes accessed | tf_op | source)
XLA Modules:
  0.0 54.5 jit_solution(8051900621385682325)
XLA Ops:
  0.0 52.2 %multislice.1 = f32[2,2,256,256]{3,2,1,0:T(8,128)} custom-call(s32[2,2]{1,0:T(2,128)} %bitcast.7, s32[2,4]{1,0:T(2,128)} %bitcast.8, s32[4]{0:T(128)} %bitcast.9, bf16[2,6,128,128]{3,2,1,0:T(8,128)(2,1)} %constant.2.clone.tab, f32[2,2,128,128]{3,2,1,0:T(8,128)} %probe_ref.1, f32[2,2,256,256]{3,2,1,0:T(8,128)} %x_ref.1, bf16[2,128,128]{2,1,0:T(8,128)(2,1)} %bitcast.6, ...), custom_call_target="tpu_custom_call" | custom-call | tf_op jit(solution)/shard_map/multislice/pallas_call | solution.py:415
  52.2 2.3 %copy.10 = f32[2,2,256,256]{3,2,1,0:T(8,128)} copy(f32[2,2,256,256]{3,2,1,0:T(8,128)} %multislice.1) | data formatting | bytes 2097152

commit v3 on v2

--- a/solution.py
+++ b/solution.py
@@ -13,6 +13,8 @@
 MARGIN = 64
 LANES = 128
 EPS = 0.1
+LEVELS = 32766.0
+TINY = 1e-30
 MESH = pl.DeviceIdType.MESH
 SIDES = ((1, 0), (-1, 0), (0, 1), (0, -1), (1, 1), (-1, 1), (1, -1), (-1, -1))
 
@@ -98,7 +100,7 @@
 
 def kernel(
     grid_shape, home_off, sur_off, helper_ref, tab, probe_ref, x_ref, home_amp, help_amp, out_ref,
-    meta, obj0, obj1, acc, pack, side, gpack, grow, gside, gcorner, amps, waves, patches,
+    meta, obj0, obj1, acc, pack, side, gpack, grow, gside, gcorner, scale_out, scale_in, amps, waves, patches,
     send_sem, recv_sem, amp_send, amp_recv,
 ):
     n_row, n_col = grid_shape
@@ -132,10 +134,21 @@
                     barrier, inc=1, device_id=(row + dr, col + dc), device_id_type=MESH
                 )
 
+    def encode(target, phase, k, strips):
+        top = functools.reduce(
+            jnp.maximum, [jnp.max(jnp.abs(v), axis=(0, 1), keepdims=True) for v in strips]
+        )
+        top = jnp.maximum(top, TINY)
+        for s, v in enumerate(strips):
+            target[k, s] = jnp.round(v * (LEVELS / top)).astype(jnp.int32).astype(jnp.int16)
+        scale_out[phase, k] = jnp.broadcast_to(top * (1.0 / LEVELS), scale_out.shape[2:])
+
+    def decode(value, phase, k, n):
+        return value.astype(jnp.int32).astype(jnp.float32) * scale_in[phase, k, n - 2, 0:1, :]
+
     for k in range(2):
         first, last = x_ref[:, k, :, 0:LANES], x_ref[:, k, :, tile - LANES:tile]
-        pack[k, 0] = pair_up(first[0], first[1], False)
-        pack[k, 1] = pair_up(last[0], last[1], True)
+        encode(pack, 0, k, [pair_up(first[0], first[1], False), pair_up(last[0], last[1], True)])
 
     vertical = jnp.where(row > 0, 1, 0) + jnp.where(row + 1 < n_row, 1, 0)
     across = 1 + jnp.where(col > 0, 1, 0) + jnp.where(col + 1 < n_col, 1, 0)
@@ -154,6 +167,11 @@
         if source == "ext":
             return slice(ext - m, ext) if d > 0 else slice(0, m)
         return slice(tile - m, tile) if d > 0 else slice(0, m)
+
+    def scale_copy(phase, k, n, target):
+        return remote(
+            scale_out.at[phase, k], scale_in.at[phase, k, n - 2], phase, k, 8 * inner + n, target
+        )
 
     def halo_copies(n, k):
         dr, dc = SIDES[n]
@@ -168,7 +186,10 @@
                 for q in range(inner)
             ]
         s = 1 if dc > 0 else 0
-        return [remote(pack.at[k, s, edge(dr, "tile")], side.at[k, 1 - s, landing], 0, k, n, target)]
+        return [
+            remote(pack.at[k, s, edge(dr, "tile")], side.at[k, 1 - s, landing], 0, k, n, target),
+            scale_copy(0, k, n, target),
+        ]
 
     def grad_copies(n, k):
         dr, dc = SIDES[n]
@@ -180,9 +201,10 @@
         s = 1 if dc > 0 else 0
         source = gpack.at[k, s, take]
         if dr == 0:
-            return [remote(source, gside.at[k, 1 - s], 1, k, n, target)]
-        u = 1 if dr > 0 else 0
-        return [remote(source, gcorner.at[k, 1 - s, 1 - u], 1, k, n, target)]
+            landing = gside.at[k, 1 - s]
+        else:
+            landing = gcorner.at[k, 1 - s, 0 if dr > 0 else 1]
+        return [remote(source, landing, 1, k, n, target), scale_copy(1, k, n, target)]
 
     def start(copies, k):
         for n, (dr, dc) in sorted(enumerate(SIDES), key=lambda e: e[1][1] == 0):
@@ -210,7 +232,7 @@
     amp_copies = [
         pltpu.make_async_remote_copy(
             src_ref=help_amp.at[h * half:(h + 1) * half],
-            dst_ref=amps.at[homes + h * half:homes + (h + 1) * half],
+            dst_ref=amps.at[h * half:(h + 1) * half],
             send_sem=amp_send.at[h], recv_sem=amp_recv.at[h],
             device_id=ring[1 - h], device_id_type=MESH,
         )
@@ -221,7 +243,7 @@
 
     for n, (dr, dc) in enumerate(SIDES):
         @pl.when(jnp.logical_not(inside(-dr, -dc)))
-        def _(dr=dr, dc=dc):
+        def _(n=n, dr=dr, dc=dc):
             landing = edge(-dr, "ext")
             u = 1 if dr > 0 else 0
             s = 1 if dc > 0 else 0
@@ -232,11 +254,13 @@
                     grow[k, 1 - u] = jnp.zeros(grow.shape[2:], jnp.float32)
                 else:
                     rows_here = landing.stop - landing.start
-                    side[k, 1 - s, landing] = jnp.zeros((rows_here, LANES), jnp.float32)
+                    side[k, 1 - s, landing] = jnp.zeros((rows_here, LANES), jnp.int16)
+                    for phase in range(2):
+                        scale_in[phase, k, n - 2] = jnp.zeros(scale_in.shape[3:], jnp.float32)
                     if dr == 0:
-                        gside[k, 1 - s] = jnp.zeros(gside.shape[2:], jnp.float32)
+                        gside[k, 1 - s] = jnp.zeros(gside.shape[2:], jnp.int16)
                     else:
-                        gcorner[k, 1 - s, 1 - u] = jnp.zeros(gcorner.shape[3:], jnp.float32)
+                        gcorner[k, 1 - s, 1 - u] = jnp.zeros(gcorner.shape[3:], jnp.int16)
 
     for h in range(homes):
         c = home_off[1, h] + (LANES - m)
@@ -252,7 +276,7 @@
         held = jnp.minimum(right * rights + left * (half + lefts), slots - 1)
         rights, lefts = rights + right, lefts + left
         c = sur_off[1, h] + (LANES - m)
-        values = (sur_off[0, h], lax.div(c, LANES), lax.rem(c, LANES), homes + held, live)
+        values = (sur_off[0, h], lax.div(c, LANES), lax.rem(c, LANES), held, live)
         for at, value in enumerate(values):
             meta[homes + h, at] = value
 
@@ -260,12 +284,17 @@
         for k in range(2):
             for q in range(inner):
                 obj[k][a, 1 + q, m:m + tile, :] = x_ref[a, k, :, q * LANES:(q + 1) * LANES]
-    amps[0:homes] = home_amp[...]
     patches[...] = jnp.zeros_like(patches)
 
     def unpack(k):
         wait_recv(halo_copies, k)
-        lower, upper = side[k, 0], side[k, 1]
+        lower, upper = (
+            jnp.concatenate(
+                [decode(side[k, s, edge(-dr, "ext")], 0, k, SIDES.index((dr, 1 - 2 * s))) for dr in (1, 0, -1)],
+                axis=0,
+            )
+            for s in range(2)
+        )
         obj[k][0, 0] = pltpu.roll(lower, LANES // 2, 1)
         obj[k][1, 0] = lower
         obj[k][0, tiles - 1] = upper
@@ -298,24 +327,25 @@
             waves[item, j, 0] = re
             waves[item, j, 1] = im
 
-    def each(fn):
+    def each(fn, begin=0):
         def step(i, carry):
             for j in range(GROUP):
                 fn(i * GROUP + j)
             return carry
 
-        lax.fori_loop(0, count // GROUP, step, 0)
+        lax.fori_loop(begin // GROUP, count // GROUP, step, 0)
 
     def enter(item):
         o1 = cut(item, 0)
         keep(item, sandwich([times(p, o1) for p in probes()], tab, 0, False))
 
-    def middle(item):
+    def middle(item, home=None):
         o2 = cut(item, 1)
         fields = kept(item)
         far = sandwich([times(b, o2) for b in fields], tab, 1, False)
         intensity = sum(re * re + im * im for re, im in far)
-        amp = amps[meta[item, 3]].astype(jnp.float32)
+        amp = amps[meta[item, 3]] if home is None else home_amp[home]
+        amp = amp.astype(jnp.float32)
         weight = 2.0 * meta[item, 4].astype(jnp.float32)
         factor = weight * (1.0 - amp * lax.rsqrt(intensity + EPS))
         exits = sandwich([(re * factor, im * factor) for re, im in far], tab, 1, True)
@@ -349,8 +379,9 @@
             return carry
 
         lax.fori_loop(0, ext // chunk, step, 0)
-        gpack[k, 0] = pair_up(acc[0, k, 0], acc[1, k, 0], True)
-        gpack[k, 1] = pair_up(acc[0, k, tiles - 1], acc[1, k, tiles - 1], False)
+        left = pair_up(acc[0, k, 0], acc[1, k, 0], True)
+        right = pair_up(acc[0, k, tiles - 1], acc[1, k, tiles - 1], False)
+        encode(gpack, 1, k, [left, right])
         start(grad_copies, k)
 
     def finish(k):
@@ -365,14 +396,12 @@
                 for s in range(2):
                     if (s == 0 and q != 0) or (s == 1 and q != inner - 1):
                         continue
-                    extra = gside[k, s]
+                    dc = 1 - 2 * s
+                    extra = decode(gside[k, s], 1, k, SIDES.index((0, dc)))
+                    top = decode(gcorner[k, s, 0], 1, k, SIDES.index((1, dc)))
+                    bottom = decode(gcorner[k, s, 1], 1, k, SIDES.index((-1, dc)))
                     extra = jnp.concatenate(
-                        [
-                            extra[:m] + gcorner[k, s, 0],
-                            extra[m:tile - m],
-                            extra[tile - m:] + gcorner[k, s, 1],
-                        ],
-                        axis=0,
+                        [extra[:m] + top, extra[m:tile - m], extra[tile - m:] + bottom], axis=0
                     )
                     if a != s:
                         extra = pltpu.roll(extra, LANES // 2, 1)
@@ -382,9 +411,11 @@
     unpack(0)
     each(enter)
     unpack(1)
+    for h in range(homes):
+        middle(h, h)
     for copy in amp_copies:
         copy.wait_recv()
-    each(middle)
+    each(middle, homes)
     gather(1)
     each(leave)
     gather(0)
@@ -422,17 +453,19 @@
             pltpu.VMEM((2, tiles, ext, LANES), f32),
             pltpu.VMEM((2, tiles, ext, LANES), f32),
             pltpu.VMEM((2, 2, tiles, ext, LANES), f32),
-            pltpu.VMEM((2, 2, tile, LANES), f32),
-            pltpu.VMEM((2, 2, ext, LANES), f32),
-            pltpu.VMEM((2, 2, ext, LANES), f32),
+            pltpu.VMEM((2, 2, tile, LANES), jnp.int16),
+            pltpu.VMEM((2, 2, ext, LANES), jnp.int16),
+            pltpu.VMEM((2, 2, ext, LANES), jnp.int16),
             pltpu.VMEM((2, 2, 2, inner, MARGIN, LANES), f32),
-            pltpu.VMEM((2, 2, tile, LANES), f32),
-            pltpu.VMEM((2, 2, 2, MARGIN, LANES), f32),
-            pltpu.VMEM((count, window, window), jnp.bfloat16),
+            pltpu.VMEM((2, 2, tile, LANES), jnp.int16),
+            pltpu.VMEM((2, 2, 2, MARGIN, LANES), jnp.int16),
+            pltpu.VMEM((2, 2, 8, LANES), f32),
+            pltpu.VMEM((2, 2, 6, 8, LANES), f32),
+            pltpu.VMEM((help_amp.shape[2], window, window), jnp.bfloat16),
             pltpu.VMEM((count, modes, 2, window, window), f32),
             pltpu.VMEM((count, 2, 2 * tile + window, LANES), f32),
-            pltpu.SemaphoreType.DMA((2, 2, 8 + 8 * (inner - 1))),
-            pltpu.SemaphoreType.DMA((2, 2, 8 + 8 * (inner - 1))),
+            pltpu.SemaphoreType.DMA((2, 2, 8 + 8 * inner)),
+            pltpu.SemaphoreType.DMA((2, 2, 8 + 8 * inner)),
             pltpu.SemaphoreType.DMA((2,)),
             pltpu.SemaphoreType.DMA((2,)),
         ],

time: 54.9 us -> 42.7 us (0.78)
  Pallas kernels: 52.2 us -> 40.3 us
    pallas_call x1, Pallas kernels: 52.2 us -> 40.3 us  [shards(): pl.pallas_call(functools.partial(kernel, grid_shape), out_shape=jax.Shape...]
where the time goes in v3:
time: 42.7 us; the launch traced here: 42.6 us
  Pallas kernels  40.3 us (94%)
  local copies, waits for them, and re-layouts  2.29 us (5%)
    pallas_call x1, Pallas kernels, shards(): pl.pallas_call(functools.partial(kernel, grid_shape), out_shape=jax.Shape...  40.3 us
    unnamed x1, local copies, waits for them, and re-layouts  2.29 us

profile of v3, /device:TPU:9, one launch (start us, length us, event | category | flops | bytes accessed | tf_op | source)
XLA Modules:
  0.0 42.6 jit_solution(15474115759958993528)
XLA Ops:
  0.0 40.3 %multislice.1 = f32[2,2,256,256]{3,2,1,0:T(8,128)} custom-call(s32[2,2]{1,0:T(2,128)} %bitcast.7, s32[2,4]{1,0:T(2,128)} %bitcast.8, s32[4]{0:T(128)} %bitcast.9, bf16[2,6,128,128]{3,2,1,0:T(8,128)(2,1)} %constant.2.clone.tab, f32[2,2,128,128]{3,2,1,0:T(8,128)} %probe_ref.1, f32[2,2,256,256]{3,2,1,0:T(8,128)} %x_ref.1, bf16[2,128,128]{2,1,0:T(8,128)(2,1)} %bitcast.6, ...), custom_call_target="tpu_custom_call" | custom-call | tf_op jit(solution)/shard_map/multislice/pallas_call | solution.py:446
  40.3 2.3 %copy.10 = f32[2,2,256,256]{3,2,1,0:T(8,128)} copy(f32[2,2,256,256]{3,2,1,0:T(8,128)} %multislice.1) | data formatting | bytes 2097152

commit v4 on v3

--- a/solution.py
+++ b/solution.py
@@ -100,7 +100,7 @@
 
 def kernel(
     grid_shape, home_off, sur_off, helper_ref, tab, probe_ref, x_ref, home_amp, help_amp, out_ref,
-    meta, obj0, obj1, acc, pack, side, gpack, grow, gside, gcorner, scale_out, scale_in, amps, waves, patches,
+    meta, obj0, obj1, acc, pack, side, gpack, grow, gside, gcorner, scale_out, scale_in, amps, waves, patches, masks,
     send_sem, recv_sem, amp_send, amp_recv,
 ):
     n_row, n_col = grid_shape
@@ -285,6 +285,12 @@
             for q in range(inner):
                 obj[k][a, 1 + q, m:m + tile, :] = x_ref[a, k, :, q * LANES:(q + 1) * LANES]
     patches[...] = jnp.zeros_like(patches)
+    lane8 = lanes((8, LANES))
+    for item in range(count):
+        begin = meta[item, 1] * LANES + meta[item, 2]
+        for t in range(tiles):
+            d = lane8 + (t * LANES - begin)
+            masks[item, t] = jnp.where((d >= 0) & (d < LANES), 1.0, 0.0)
 
     def unpack(k):
         wait_recv(halo_copies, k)
@@ -328,52 +334,56 @@
             waves[item, j, 1] = im
 
     def each(fn, begin=0):
+        group = next(g for g in SIZES if (count - begin) % g == 0)
+
         def step(i, carry):
-            for j in range(GROUP):
-                fn(i * GROUP + j)
+            fn([begin + i * group + j for j in range(group)])
             return carry
 
-        lax.fori_loop(begin // GROUP, count // GROUP, step, 0)
-
-    def enter(item):
-        o1 = cut(item, 0)
-        keep(item, sandwich([times(p, o1) for p in probes()], tab, 0, False))
-
-    def middle(item, home=None):
-        o2 = cut(item, 1)
-        fields = kept(item)
-        far = sandwich([times(b, o2) for b in fields], tab, 1, False)
-        intensity = sum(re * re + im * im for re, im in far)
-        amp = amps[meta[item, 3]] if home is None else home_amp[home]
-        amp = amp.astype(jnp.float32)
-        weight = 2.0 * meta[item, 4].astype(jnp.float32)
-        factor = weight * (1.0 - amp * lax.rsqrt(intensity + EPS))
-        exits = sandwich([(re * factor, im * factor) for re, im in far], tab, 1, True)
-        put(item, total([conj_times(b, e) for b, e in zip(fields, exits)]))
-        keep(item, [conj_times(o2, e) for e in exits])
-
-    def leave(item):
-        entry = sandwich(kept(item), tab, 0, True)
-        put(item, total([conj_times(p, e) for p, e in zip(probes(), entry)]))
+        lax.fori_loop(0, (count - begin) // group, step, 0)
+
+    def joint(groups, which, conj):
+        flat = sandwich([f for fields in groups for f in fields], tab, which, conj)
+        return [flat[i * modes:(i + 1) * modes] for i in range(len(groups))]
+
+    def enter(items):
+        waves_in = []
+        for item in items:
+            o1 = cut(item, 0)
+            waves_in.append([times(p, o1) for p in probes()])
+        for item, fields in zip(items, joint(waves_in, 0, False)):
+            keep(item, fields)
+
+    def middle(items, home=False):
+        o2s = [cut(item, 1) for item in items]
+        fields = [[times(b, o2) for b in kept(item)] for item, o2 in zip(items, o2s)]
+        seen = []
+        for item, far in zip(items, joint(fields, 1, False)):
+            intensity = sum(re * re + im * im for re, im in far)
+            amp = home_amp[item] if home else amps[meta[item, 3]]
+            weight = 2.0 * meta[item, 4].astype(jnp.float32)
+            factor = weight * (1.0 - amp.astype(jnp.float32) * lax.rsqrt(intensity + EPS))
+            seen.append([(re * factor, im * factor) for re, im in far])
+        for item, o2, exits in zip(items, o2s, joint(seen, 1, True)):
+            put(item, total([conj_times(b, e) for b, e in zip(kept(item), exits)]))
+            keep(item, [conj_times(o2, e) for e in exits])
+
+    def leave(items):
+        for item, entry in zip(items, joint([kept(item) for item in items], 0, True)):
+            put(item, total([conj_times(p, e) for p, e in zip(probes(), entry)]))
 
     chunk = 32
 
     def gather(k):
-        lane8 = lanes((chunk, LANES))
-
         def step(i, carry):
             begin = pl.multiple_of(i * chunk, chunk)
             for a in range(2):
                 sums = [jnp.zeros((chunk, LANES), jnp.float32) for _ in range(tiles)]
                 for item in range(count):
-                    at, q, shift = meta[item, 0], meta[item, 1], meta[item, 2]
-                    piece = patches[item, a, pl.ds(tile - at + begin, chunk), :]
-                    high = jnp.where(lane8 >= shift, piece, 0.0)
-                    low = piece - high
+                    piece = patches[item, a, pl.ds(tile - meta[item, 0] + begin, chunk), :]
                     for t in range(tiles):
-                        hit = jnp.where(q == t, 1.0, 0.0)
-                        miss = jnp.where(q + 1 == t, 1.0, 0.0)
-                        sums[t] = sums[t] + (high * hit + low * miss)
+                        mask = jnp.concatenate([masks[item, t]] * (chunk // 8), axis=0)
+                        sums[t] = sums[t] + piece * mask
                 for t in range(tiles):
                     acc[a, k, t, pl.ds(begin, chunk), :] = sums[t]
             return carry
@@ -411,8 +421,7 @@
     unpack(0)
     each(enter)
     unpack(1)
-    for h in range(homes):
-        middle(h, h)
+    middle(list(range(homes)), True)
     for copy in amp_copies:
         copy.wait_recv()
     each(middle, homes)
@@ -428,7 +437,7 @@
         copy.wait_send()
 
 
-GROUP = 2
+SIZES = (4, 3, 2, 1)
 
 
 def shards(object_tiles, probe_modes, home_offset, home_amp, sur_offset, sur_helper, help_amp):
@@ -464,6 +473,7 @@
             pltpu.VMEM((help_amp.shape[2], window, window), jnp.bfloat16),
             pltpu.VMEM((count, modes, 2, window, window), f32),
             pltpu.VMEM((count, 2, 2 * tile + window, LANES), f32),
+            pltpu.VMEM((count, tiles, 8, LANES), f32),
             pltpu.SemaphoreType.DMA((2, 2, 8 + 8 * inner)),
             pltpu.SemaphoreType.DMA((2, 2, 8 + 8 * inner)),
             pltpu.SemaphoreType.DMA((2,)),

time: 42.7 us -> 39.6 us (0.927)
  Pallas kernels: 40.3 us -> 37.1 us
    pallas_call x1, Pallas kernels: 40.3 us -> 37.1 us  [shards(): pl.pallas_call(functools.partial(kernel, grid_shape), out_shape=jax.Shape...]
where the time goes in v4:
time: 39.6 us; the launch traced here: 39.4 us
  Pallas kernels  37.1 us (94%)
  local copies, waits for them, and re-layouts  2.29 us (6%)
    pallas_call x1, Pallas kernels, shards(): pl.pallas_call(functools.partial(kernel, grid_shape), out_shape=jax.Shape...  37.1 us
    unnamed x1, local copies, waits for them, and re-layouts  2.29 us

profile of v4, /device:TPU:9, one launch (start us, length us, event | category | flops | bytes accessed | tf_op | source)
XLA Modules:
  0.0 39.4 jit_solution(14943253912260171962)
XLA Ops:
  0.0 37.1 %multislice.1 = f32[2,2,256,256]{3,2,1,0:T(8,128)} custom-call(s32[2,2]{1,0:T(2,128)} %bitcast.7, s32[2,4]{1,0:T(2,128)} %bitcast.8, s32[4]{0:T(128)} %bitcast.9, bf16[2,6,128,128]{3,2,1,0:T(8,128)(2,1)} %constant.2.clone.tab, f32[2,2,128,128]{3,2,1,0:T(8,128)} %probe_ref.1, f32[2,2,256,256]{3,2,1,0:T(8,128)} %x_ref.1, bf16[2,128,128]{2,1,0:T(8,128)(2,1)} %bitcast.6, ...), custom_call_target="tpu_custom_call" | custom-call | tf_op jit(solution)/shard_map/multislice/pallas_call | solution.py:455
  37.1 2.3 %copy.10 = f32[2,2,256,256]{3,2,1,0:T(8,128)} copy(f32[2,2,256,256]{3,2,1,0:T(8,128)} %multislice.1) | data formatting | bytes 2097152
